TPU v7x, 128 devices: a whole 4x4x4 slice. The times are simulated.
128 devices in a mesh: pipe: 4 (over z), seq: 16 (over y, x), cfg: 2 (over core).
Axes of the slice: x: 4, y: 4, z: 4, core: 2. Of those that a mesh axis runs over, the one named last changes fastest.
Arguments:
- hidden: bfloat16 [2, 4, 2048, 5120], P('cfg', 'pipe', 'seq'), may hold values from -6 to 6
- qkv_weight: bfloat16 [4, 5120, 3, 4096], P('pipe', None, None, 'seq'), may hold values from -1 to 1
- out_weight: bfloat16 [4, 4096, 5120], P('pipe', 'seq'), may hold values from -0.09375 to 0.09375
- qk_gain: float32 [4, 2, 4096], P('pipe', None, 'seq'), may hold values from 0 to 8
- stale_kv: bfloat16 [2, 4, 2, 4096, 4096], P('cfg', 'pipe', None, None, 'seq'), may hold values from -6 to 6
- modulation: float32 [4, 50, 3, 5120], P('pipe'), may hold values from -3 to 3
- head_mod: float32 [50, 2, 5120], replicated, may hold values from -3 to 3
- head_weight: bfloat16 [5120, 64], replicated, may hold values from -0.078125 to 0.078125
- patch_index: int32 [1], replicated, may hold values from 0 to 1
- timestep: int32 [1], replicated, may hold values from 0 to 49
Outputs:
- forwarded: bfloat16 [2, 4, 2048, 5120], P('cfg', 'pipe', 'seq')
- fresh_kv: bfloat16 [2, 4, 2, 2048, 4096], P('cfg', 'pipe', None, None, 'seq')
- guided: float32 [4, 2048, 64], P('pipe', 'seq', 'cfg')
All inputs are finite; a program needn't handle non-finite values.
Results may differ from a plain program's by a relative error of at most 0.01.
Values may be sent and summed in bfloat16 or wider, within the bound.
No kernel may reach another device: no remote copies, remote signals or barrier semaphores. Data moves between devices by JAX's collectives and lax.ppermute only.
A program may use at most 128 MiB of HBM per device.

v0:
```python
import math

import jax
import jax.numpy as jnp
from jax import lax
from jax.sharding import PartitionSpec as P

HEAD = 128
NPATCH = 2


epsilon = 1e-06
guidance = 5.0


def passed_along(block, axis, distance):
    devices = range(lax.axis_size(axis))
    route = [((i - distance) % len(devices), i) for i in devices]
    return lax.ppermute(block, axis, route)


def partner_2(shard, axis, stride):
    return lax.ppermute(shard, axis, [(i, i ^ 1 << stride) for i in range(lax.axis_size(axis))])


def modulate(inputs, shift_row, scale_row):
    values = inputs.astype(jnp.float32)
    center = jnp.mean(values, axis=-1, keepdims=True)
    spread = jnp.mean(jnp.square(values - center), axis=-1, keepdims=True)
    return (values - center) * lax.rsqrt(spread + epsilon) * (1.0 + scale_row) + shift_row


def per_device(
    hidden,
    qkv_weight,
    out_weight,
    qk_gain,
    stale_kv,
    modulation,
    head_mod,
    head_weight,
    patch_index,
    timestep,
):
    tokens_in = hidden[0, 0]
    step_row = timestep[0]
    mod_rows = lax.dynamic_index_in_dim(modulation[0], step_row, 0, keepdims=False)
    head_rows = lax.dynamic_index_in_dim(head_mod, step_row, 0, keepdims=False)
    in_weight = qkv_weight[0]
    model_width = in_weight.shape[0]
    local_width = in_weight.shape[2]
    in_weight = in_weight.reshape(model_width, 3 * local_width)
    normed = modulate(tokens_in, mod_rows[0], mod_rows[1]).astype(jnp.bfloat16)
    projections = jnp.dot(
        lax.all_gather(normed, "seq", axis=0, tiled=True),
        in_weight,
        preferred_element_type=jnp.float32,
    )
    patch_tokens = projections.shape[0]
    queries = projections[:, :local_width]
    key_cols = projections[:, local_width : 2 * local_width]
    value_cols = projections[:, 2 * local_width :]
    square_sums = lax.psum(
        (jnp.sum(jnp.square(queries), axis=-1), jnp.sum(jnp.square(key_cols), axis=-1)), "seq"
    )
    full_width = local_width * lax.axis_size("seq")
    qk_gains = qk_gain[0]
    query_scale = lax.rsqrt(square_sums[0] / full_width + epsilon)[:, None]
    key_scale = lax.rsqrt(square_sums[1] / full_width + epsilon)[:, None]
    query_normed = (queries * query_scale * qk_gains[0]).astype(jnp.bfloat16)
    key_normed = (key_cols * key_scale * qk_gains[1]).astype(jnp.bfloat16)
    value_normed = value_cols.astype(jnp.bfloat16)
    section_index = lax.axis_index("pipe")
    patch_slot = jnp.mod(patch_index[0] - section_index, NPATCH)
    first_row = patch_slot * patch_tokens
    key_set = lax.dynamic_update_slice(stale_kv[0, 0, 0], key_normed, (first_row, jnp.int32(0)))
    value_set = lax.dynamic_update_slice(stale_kv[0, 0, 1], value_normed, (first_row, jnp.int32(0)))
    seq_rows = key_set.shape[0]
    heads_here = local_width // HEAD
    key_heads = key_set.reshape(seq_rows, heads_here, HEAD)
    value_heads = value_set.reshape(seq_rows, heads_here, HEAD)
    block_rows = math.gcd(patch_tokens, 512)
    block_count = patch_tokens // block_rows

    def attend(query_block):
        scores = jnp.einsum(
            "qhc,khc->hqk", query_block, key_heads, preferred_element_type=jnp.float32
        ) * HEAD ** (-0.5)
        top = jnp.max(scores, axis=-1, keepdims=True)
        expo = jnp.exp(scores - top)
        weights = (expo / jnp.sum(expo, axis=-1, keepdims=True)).astype(jnp.bfloat16)
        mixed = jnp.einsum("hqk,khc->qhc", weights, value_heads, preferred_element_type=jnp.float32)
        return mixed.astype(jnp.bfloat16).reshape(block_rows, local_width)

    attended = lax.map(attend, query_normed.reshape(block_count, block_rows, heads_here, HEAD))
    attended = attended.reshape(patch_tokens, local_width)
    out_rows = out_weight[0]
    projected = lax.psum_scatter(
        jnp.dot(attended, out_rows, preferred_element_type=jnp.float32).astype(jnp.bfloat16),
        "seq",
        scatter_dimension=0,
        tiled=True,
    ).astype(jnp.float32)
    block_out = (tokens_in.astype(jnp.float32) + mod_rows[2] * projected).astype(jnp.bfloat16)
    forwarded = passed_along(block_out, "pipe", 1)
    normed_out = modulate(block_out, head_rows[0], head_rows[1]).astype(jnp.bfloat16)
    readout = jnp.dot(normed_out, head_weight, preferred_element_type=jnp.float32)
    branch_index = lax.axis_index("cfg")
    half_width = readout.shape[1] // 2
    partner = partner_2(readout.astype(jnp.bfloat16), "cfg", 0).astype(readout.dtype)
    conditional = jnp.where(branch_index == 0, readout, partner)
    unconditional = jnp.where(branch_index == 0, partner, readout)
    combined = unconditional + guidance * (conditional - unconditional)
    guided = lax.dynamic_slice_in_dim(combined, branch_index * half_width, half_width, 1)
    fresh_pair = jnp.stack([key_normed, value_normed])
    return (forwarded[None, None], fresh_pair[None, None], guided[None])


def solution(mesh):
    return jax.shard_map(
        per_device,
        mesh=mesh,
        in_specs=(
            P("cfg", "pipe", "seq", None),
            P("pipe", None, None, "seq"),
            P("pipe", "seq", None),
            P("pipe", None, "seq"),
            P("cfg", "pipe", None, None, "seq"),
            P("pipe", None, None, None),
            P(),
            P(),
            P(),
            P(),
        ),
        out_specs=(
            P("cfg", "pipe", "seq", None),
            P("cfg", "pipe", None, None, "seq"),
            P("pipe", "seq", "cfg"),
        ),
        check_vma=False,
    )
```

profile of v0, /device:TPU:0, one launch (start us, length us, event | category | flops | bytes accessed | tf_op | source)
XLA Modules:
  0.0 539.0 jit_solution(13400286598347990033)
XLA Ops:
  16.5 10.7 %copy.18 = bf16[1,5120,3,256]{1,3,2,0:T(8,128)(2,1)} copy(bf16[1,5120,3,256]{3,1,2,0:T(8,128)(2,1)} %param.13) | data formatting | bytes 15728640 | tf_op args[1]
  27.3 5.1 slice_bitcast_fusion
  32.4 4.1 copy.28
  36.5 114.6 %all-gather.2.cloned.1.call-done = bf16[2048,5120]{1,0:T(8,128)(2,1)} async-done(((bf16[128,5120]{1,0:T(8,128)(2,1)}), bf16[2048,5120]{1,0:T(8,128)(2,1)}) %all-gather.2.cloned.1.call-update) | async-done | bytes 20971536 | tf_op jit(solution)/shard_map/all_gather | solution.py:55
  151.0 20.4 %fusion.57 = f32[2048,768]{0,1:T(8,128)S(1)} fusion(bf16[2048,5120]{1,0:T(8,128)(2,1)} %all-gather.2.cloned.1.call-done, bf16[5120,768]{0,1:T(8,128)(2,1)} %bitcast.88), kind=kOutput, calls=%fused_computation.71 | convolution fusion | flops 16106127360 | bytes 35127296 | tf_op jit(solution)/shard_map/dot_general | solution.py:54
  174.5 72.4 %all-reduce = (f32[2048]{0:T(1024)S(1)}, f32[2048]{0:T(1024)S(1)}) all-reduce(f32[2048]{0:T(1024)S(1)} %get-tuple-element.48, f32[2048]{0:T(1024)S(1)} %get-tuple-element.47), channel_id=1, replica_groups=mesh['pipe'=4,'seq'=16,'cfg'=2] {'seq'}, use_global_device_ids=true, to_apply=%region_3.4 | all-reduce | flops 4096 | bytes 32768 | tf_op jit(solution)/shard_map/psum | solution.py:63
  246.9 3.8 fusion.54
  255.2 4.1 copy.21
  259.3 4.1 copy.23
  263.4 4.0 fusion.47
  272.7 82.0 %while.10 = (s32[]{:T(128)}, bf16[4,512,256]{2,1,0:T(8,128)(2,1)}, bf16[4,512,2,128]{3,1,2,0:T(8,128)(2,1)}, bf16[4096,2,128]{2,0,1:T(8,128)(2,1)}, bf16[4096,2,128]{0,2,1:T(8,128)(2,1)}, /*index=5*/s32[]{:T(128)}) while((s32[]{:T(128)}, bf16[4,512,256]{2,1,0:T(8,128)(2,1)}, bf16[4,512,2,128]{3,1,2,0:T(8,128)(2,1)}, ...), condition=%wide.region_9.10_spmd, body=%wide.region_6.9_spmd.sunk | while | flops 2168590336 | bytes 39330884 | solution.py:95
  272.7 10.3 %fusion.73 = (f32[2,512]{1,0:T(2,128)S(1)}, f32[2,512,4096]{2,1,0:T(8,128)}) fusion(bf16[4096,2,128]{2,0,1:T(8,128)(2,1)} %get-tuple-element.132, bf16[4,512,2,128]{3,1,2,0:T(8,128)(2,1)} %get-tuple-element.131, s32[]{:T(128)} %get-tuple-element.123), kind=kOutput, calls=%fused_computation.67.clone.1 | convolution fusion | flops 1086328832 | bytes 19141120 | tf_op jit(solution)/shard_map/while/body/eval_jaxpr/sub | solution.py:90
  282.9 9.3 %fusion.74 = bf16[2,512,128]{1,2,0:T(8,128)(2,1)S(1)} fusion(bf16[4096,2,128]{0,2,1:T(8,128)(2,1)} %get-tuple-element.133, f32[2,512,4096]{2,1,0:T(8,128)} %get-tuple-element.115, f32[2,512]{1,0:T(2,128)S(1)} %get-tuple-element.116), kind=kOutput, calls=%fused_computation.8.clone.1 | convolution fusion | flops 1082261504 | bytes 19140608 | tf_op jit(solution)/shard_map/while/body/eval_jaxpr/hqk,khc->qhc/dot_general | solution.py:92
  293.2 10.3 %fusion.73 = (f32[2,512]{1,0:T(2,128)S(1)}, f32[2,512,4096]{2,1,0:T(8,128)}) fusion(bf16[4096,2,128]{2,0,1:T(8,128)(2,1)} %get-tuple-element.132, bf16[4,512,2,128]{3,1,2,0:T(8,128)(2,1)} %get-tuple-element.131, s32[]{:T(128)} %get-tuple-element.123), kind=kOutput, calls=%fused_computation.67.clone.1 | convolution fusion | flops 1086328832 | bytes 19141120 | tf_op jit(solution)/shard_map/while/body/eval_jaxpr/sub | solution.py:90
  303.4 9.3 %fusion.74 = bf16[2,512,128]{1,2,0:T(8,128)(2,1)S(1)} fusion(bf16[4096,2,128]{0,2,1:T(8,128)(2,1)} %get-tuple-element.133, f32[2,512,4096]{2,1,0:T(8,128)} %get-tuple-element.115, f32[2,512]{1,0:T(2,128)S(1)} %get-tuple-element.116), kind=kOutput, calls=%fused_computation.8.clone.1 | convolution fusion | flops 1082261504 | bytes 19140608 | tf_op jit(solution)/shard_map/while/body/eval_jaxpr/hqk,khc->qhc/dot_general | solution.py:92
  313.7 10.3 %fusion.73 = (f32[2,512]{1,0:T(2,128)S(1)}, f32[2,512,4096]{2,1,0:T(8,128)}) fusion(bf16[4096,2,128]{2,0,1:T(8,128)(2,1)} %get-tuple-element.132, bf16[4,512,2,128]{3,1,2,0:T(8,128)(2,1)} %get-tuple-element.131, s32[]{:T(128)} %get-tuple-element.123), kind=kOutput, calls=%fused_computation.67.clone.1 | convolution fusion | flops 1086328832 | bytes 19141120 | tf_op jit(solution)/shard_map/while/body/eval_jaxpr/sub | solution.py:90
  323.9 9.3 %fusion.74 = bf16[2,512,128]{1,2,0:T(8,128)(2,1)S(1)} fusion(bf16[4096,2,128]{0,2,1:T(8,128)(2,1)} %get-tuple-element.133, f32[2,512,4096]{2,1,0:T(8,128)} %get-tuple-element.115, f32[2,512]{1,0:T(2,128)S(1)} %get-tuple-element.116), kind=kOutput, calls=%fused_computation.8.clone.1 | convolution fusion | flops 1082261504 | bytes 19140608 | tf_op jit(solution)/shard_map/while/body/eval_jaxpr/hqk,khc->qhc/dot_general | solution.py:92
  334.1 10.3 %fusion.73 = (f32[2,512]{1,0:T(2,128)S(1)}, f32[2,512,4096]{2,1,0:T(8,128)}) fusion(bf16[4096,2,128]{2,0,1:T(8,128)(2,1)} %get-tuple-element.132, bf16[4,512,2,128]{3,1,2,0:T(8,128)(2,1)} %get-tuple-element.131, s32[]{:T(128)} %get-tuple-element.123), kind=kOutput, calls=%fused_computation.67.clone.1 | convolution fusion | flops 1086328832 | bytes 19141120 | tf_op jit(solution)/shard_map/while/body/eval_jaxpr/sub | solution.py:90
  344.4 9.4 %fusion.74 = bf16[2,512,128]{1,2,0:T(8,128)(2,1)S(1)} fusion(bf16[4096,2,128]{0,2,1:T(8,128)(2,1)} %get-tuple-element.133, f32[2,512,4096]{2,1,0:T(8,128)} %get-tuple-element.115, f32[2,512]{1,0:T(2,128)S(1)} %get-tuple-element.116), kind=kOutput, calls=%fused_computation.8.clone.1 | convolution fusion | flops 1082261504 | bytes 19140608 | tf_op jit(solution)/shard_map/while/body/eval_jaxpr/hqk,khc->qhc/dot_general | solution.py:92
  354.6 11.2 %convolution_convert_fusion = bf16[2048,5120]{1,0:T(8,128)(2,1)} fusion(bf16[2048,256]{1,0:T(8,128)(2,1)} %bitcast.91, bf16[1,256,5120]{2,1,0:T(8,128)(2,1)S(1)} %copy-done), kind=kOutput, calls=%fused_computation.18 | convolution fusion | flops 5379194880 | bytes 24641536 | tf_op jit(solution)/shard_map/dot_general | solution.py:99
  366.8 127.4 %reduce-scatter.2.cloned.1.call-done = bf16[128,5120]{1,0:T(8,128)(2,1)} async-done(((bf16[2048,5120]{1,0:T(8,128)(2,1)}), bf16[128,5120]{1,0:T(8,128)(2,1)}) %reduce-scatter.2.cloned.1.call-update) | async-done | bytes 1310736 | tf_op jit(solution)/shard_map/reduce_scatter | solution.py:98
  494.2 3.3 convert_reduce_fusion
  504.8 3.9 copy.25
  509.4 20.3 %collective-permute-done = bf16[128,5120]{1,0:T(8,128)(2,1)} collective-permute-done((bf16[128,5120]{1,0:T(8,128)(2,1)}, bf16[128,5120]{1,0:T(8,128)(2,1)}, u32[]{:S(2)}, u32[]{:S(2)}) %collective-permute-start) | collective-permute-done | bytes 1310752 | tf_op jit(solution)/shard_map/ppermute | solution.py:19
  (51 shorter events, 35.4 us)
Async XLA Ops:
  7.2 347.5 %copy-start = (bf16[1,256,5120]{2,1,0:T(8,128)(2,1)S(1)}, bf16[1,256,5120]{2,1,0:T(8,128)(2,1)}, u32[]{:S(2)}) copy-start(bf16[1,256,5120]{2,1,0:T(8,128)(2,1)} %param.14) | copy-start | bytes 7864324
  7.2 143.8 %all-gather.2.cloned.1.call-start = ((), (), s32[]{:S(2)}) async-start(), calls=%async_computation.1 | async-start | bytes 22282240 | tf_op jit(solution)/shard_map/all_gather | solution.py:55
  15.8 478.4 %reduce-scatter.2.cloned.1.call-start = ((), (), s32[]{:S(2)}) async-start(), calls=%async_computation.2 | async-start | bytes 22282240 | tf_op jit(solution)/shard_map/reduce_scatter | solution.py:98
  32.4 4.1 copy-start.5
  171.4 2.7 copy-start.1
  365.9 128.4 %copy-start.4 = (f32[1,1,1,5120]{3,0,2,1:T(1,128)S(1)}, f32[1,1,1,5120]{3,0,2,1:T(1,128)}, u32[]{:S(2)}) copy-start(f32[1,1,1,5120]{3,0,2,1:T(1,128)} %get-tuple-element.71) | copy-start | bytes 61444
  494.2 6.8 %copy-start.6 = (bf16[5120,64]{0,1:T(8,128)(2,1)S(1)}, bf16[5120,64]{0,1:T(8,128)(2,1)}, u32[]{:S(2)}) copy-start(bf16[5120,64]{0,1:T(8,128)(2,1)} %param.19) | copy-start | bytes 1966084
  497.5 32.1 %collective-permute-start = (bf16[128,5120]{1,0:T(8,128)(2,1)}, bf16[128,5120]{1,0:T(8,128)(2,1)}, u32[]{:S(2)}, u32[]{:S(2)}) collective-permute-start(bf16[128,5120]{1,0:T(8,128)(2,1)} %get-tuple-element.62), channel_id=1, source_target_pairs={{96,0},{0,32},{32,64},{64,96},{97,1},{1,33},{33,65},{65,97},{98,2}... | collective-permute-start | bytes 3932168 | tf_op jit(solution)/shard_map/ppermute | solution.py:19
  499.1 4.2 copy-start.2
  499.1 4.2 copy-start.3
  503.2 5.6 %collective-permute-start.1 = (bf16[128,64]{0,1:T(8,128)(2,1)S(1)}, bf16[128,64]{0,1:T(8,128)(2,1)S(1)}, u32[]{:S(2)}, u32[]{:S(2)}) collective-permute-start(bf16[128,64]{0,1:T(8,128)(2,1)S(1)} %get-tuple-element.78), channel_id=1, source_target_pairs={{0,1},{1,0},{2,3},{3,2},{4,5},{5,4},{6,7},{7,6},{8,9},{9,8},{10,11... | collective-permute-start | bytes 49160 | tf_op jit(solution)/shard_map/ppermute | solution.py:23
Sparse Core Ops, SparseCore 0:
  15.9 135.0 all-gather.1
  366.0 128.1 reduce-scatter.1
where the time goes:
time: 540 us; the launch traced here: 539 us
  waiting for transfers between devices  262 us (49%)
  matrix products  112 us (21%)
  blocking collectives  72.4 us (13%)
  local copies, waits for them, and re-layouts  50.4 us (9%)
  other arithmetic  24.3 us (4%)
  between operations  15.6 us (3%)
    reduce_scatter x1, waiting for transfers between devices, per_device(): lax.psum_scatter(jnp.dot(attended, out_rows, preferred_element_type=jnp.f...  127 us
    all_gather x1, waiting for transfers between devices, per_device(): lax.all_gather(normed, 'seq', axis=0, tiled=True)  115 us
    psum x1, blocking collectives, per_device(): lax.psum((jnp.sum(jnp.square(queries), axis=-1), jnp.sum(jnp.square(key_c...  72.4 us
    sub x4, matrix products, attend(): expo = jnp.exp(scores - top)  41.1 us
    dot_general x4, matrix products, attend(): jnp.einsum('hqk,khc->qhc', weights, value_heads, preferred_element_type=j...  37.4 us
    unnamed x18, local copies, waits for them, and re-layouts  23.9 us
    dot_general x1, matrix products, per_device(): jnp.dot(lax.all_gather(normed, 'seq', axis=0, tiled=True), in_weight, pre...  20.4 us
    ppermute x1, waiting for transfers between devices, passed_along(): return lax.ppermute(block, axis, route)  20.3 us
  transfers between devices with their start and end apart: 4, of which 3 were waited for; matrix products, arithmetic and copies ran while one was open for 6% of the time, Pallas kernels for 0%

commit v1 on v0

v1 whole, which is shorter than its diff:
```python
import functools
import math

import jax
import jax.numpy as jnp
from jax import lax
from jax.experimental import pallas as pl
from jax.experimental.pallas import tpu as pltpu
from jax.sharding import Mesh, PartitionSpec as P

HEAD = 128
NPATCH = 2
epsilon = 1e-06
guidance = 5.0
SCORE = math.log2(math.e) * HEAD**-0.5
LAST = (((1,), (1,)), ((), ()))


def passed_along(block, axis, distance):
    devices = range(lax.axis_size(axis))
    route = [((i - distance) % len(devices), i) for i in devices]
    return lax.ppermute(block, axis, route)


def partner_2(shard, axis, stride):
    return lax.ppermute(shard, axis, [(i, i ^ stride) for i in range(lax.axis_size(axis))])


def butterfly_sum(value):
    for axis in ("x", "y"):
        for stride in (1, 2):
            value = value + partner_2(value, axis, stride)
    return value


def modulate(inputs, shift_row, scale_row):
    values = inputs.astype(jnp.float32)
    center = jnp.mean(values, axis=-1, keepdims=True)
    spread = jnp.mean(jnp.square(values - center), axis=-1, keepdims=True)
    return (values - center) * lax.rsqrt(spread + epsilon) * (1.0 + scale_row) + shift_row


def norm_body(step_ref, x_ref, mod_ref, out_ref):
    out_ref[...] = modulate(x_ref[...], mod_ref[0, 0:1, :], mod_ref[0, 1:2, :]).astype(
        jnp.bfloat16
    )


def norm_rows(timestep, tokens, table):
    rows, width = tokens.shape
    part = rows // 4
    return pl.pallas_call(
        norm_body,
        grid_spec=pltpu.PrefetchScalarGridSpec(
            num_scalar_prefetch=1,
            grid=(4,),
            in_specs=[
                pl.BlockSpec((part, width), lambda i, t: (i, 0)),
                pl.BlockSpec((1,) + table.shape[1:], lambda i, t: (t[0], 0, 0)),
            ],
            out_specs=pl.BlockSpec((part, width), lambda i, t: (i, 0)),
        ),
        out_shape=jax.ShapeDtypeStruct((rows, width), jnp.bfloat16),
    )(timestep, tokens, table)


def attend_body(slot_ref, q_ref, kf, vf, ks, vs, out_ref):
    queries = q_ref[...]
    top = total = mixed = None
    for keys, values in ((kf, vf), (ks, vs)):
        scores = lax.dot_general(queries, keys[0], LAST, preferred_element_type=jnp.float32)
        high = jnp.max(scores, axis=-1, keepdims=True) * SCORE
        new_top = high if top is None else jnp.maximum(top, high)
        expo = jnp.exp2(scores * SCORE - new_top)
        part = jnp.sum(expo, axis=-1, keepdims=True)
        term = jnp.dot(expo.astype(jnp.bfloat16), values[0], preferred_element_type=jnp.float32)
        if top is None:
            total, mixed = part, term
        else:
            decay = jnp.exp2(top - new_top)
            total, mixed = total * decay + part, mixed * decay + term
        top = new_top
    out_ref[...] = (mixed / total).astype(jnp.bfloat16)


def attend(other_slot, queries, fresh, stale, block):
    rows, width = queries.shape
    keys = fresh.shape[1]
    return pl.pallas_call(
        attend_body,
        grid_spec=pltpu.PrefetchScalarGridSpec(
            num_scalar_prefetch=1,
            grid=(width // HEAD, rows // block),
            in_specs=[
                pl.BlockSpec((block, HEAD), lambda h, i, s: (i, h)),
                pl.BlockSpec((1, keys, HEAD), lambda h, i, s: (0, 0, h)),
                pl.BlockSpec((1, keys, HEAD), lambda h, i, s: (1, 0, h)),
                pl.BlockSpec((1, keys, HEAD), lambda h, i, s: (0, s[0], h)),
                pl.BlockSpec((1, keys, HEAD), lambda h, i, s: (1, s[0], h)),
            ],
            out_specs=pl.BlockSpec((block, HEAD), lambda h, i, s: (i, h)),
        ),
        out_shape=jax.ShapeDtypeStruct((rows, width), jnp.bfloat16),
        compiler_params=pltpu.CompilerParams(vmem_limit_bytes=56 * 2**20),
        cost_estimate=pl.CostEstimate(
            flops=8 * rows * keys * width,
            bytes_accessed=8 * keys * width,
            transcendentals=4 * rows * keys,
        ),
    )(other_slot, queries, fresh, fresh, stale, stale)


def per_device(
    hidden,
    qkv_weight,
    out_weight,
    qk_gain,
    stale_kv,
    modulation,
    head_mod,
    head_weight,
    patch_index,
    timestep,
):
    tokens_in = hidden[0, 0]
    step_row = timestep[0]
    in_weight = qkv_weight[0]
    model_width = in_weight.shape[0]
    local_width = in_weight.shape[2]
    in_weight = in_weight.reshape(model_width, 3 * local_width)
    normed = norm_rows(timestep, tokens_in, modulation[0])
    gathered = lax.all_gather(normed, ("y", "x"), axis=0, tiled=True)
    projections = jnp.dot(gathered, in_weight, preferred_element_type=jnp.float32)
    queries = projections[:, :local_width]
    key_cols = projections[:, local_width : 2 * local_width]
    value_cols = projections[:, 2 * local_width :]
    square_sums = butterfly_sum(
        jnp.stack([jnp.sum(jnp.square(queries), -1), jnp.sum(jnp.square(key_cols), -1)])
    )
    full_width = local_width * lax.axis_size(("y", "x"))
    scales = lax.rsqrt(square_sums / full_width + epsilon)[:, :, None]
    query_normed = (queries * scales[0] * qk_gain[0, 0]).astype(jnp.bfloat16)
    key_normed = (key_cols * scales[1] * qk_gain[0, 1]).astype(jnp.bfloat16)
    fresh_pair = jnp.stack([key_normed, value_cols.astype(jnp.bfloat16)])
    patch_slot = jnp.mod(patch_index - lax.axis_index("pipe"), NPATCH)
    attended = attend(1 - patch_slot, query_normed, fresh_pair, stale_kv[0, 0], 512)
    projected = lax.psum_scatter(
        jnp.dot(attended, out_weight[0], preferred_element_type=jnp.float32).astype(jnp.bfloat16),
        ("y", "x"),
        scatter_dimension=0,
        tiled=True,
    ).astype(jnp.float32)
    gate = lax.dynamic_slice(modulation[0], (step_row, 2, 0), (1, 1, model_width))[0]
    block_out = (tokens_in.astype(jnp.float32) + gate * projected).astype(jnp.bfloat16)
    forwarded = passed_along(block_out, "pipe", 1)
    head_rows = lax.dynamic_index_in_dim(head_mod, step_row, 0, keepdims=False)
    normed_out = modulate(block_out, head_rows[0], head_rows[1]).astype(jnp.bfloat16)
    readout = jnp.dot(normed_out, head_weight, preferred_element_type=jnp.float32)
    branch_index = lax.axis_index("cfg")
    half_width = readout.shape[1] // 2
    partner = partner_2(readout.astype(jnp.bfloat16), "cfg", 1).astype(readout.dtype)
    conditional = jnp.where(branch_index == 0, readout, partner)
    unconditional = jnp.where(branch_index == 0, partner, readout)
    combined = unconditional + guidance * (conditional - unconditional)
    guided = lax.dynamic_slice_in_dim(combined, branch_index * half_width, half_width, 1)
    return (forwarded[None, None], fresh_pair[None, None], guided[None])


def solution(mesh):
    sizes = (mesh.shape["pipe"], 4, mesh.shape["seq"] // 4, mesh.shape["cfg"])
    grid = Mesh(mesh.devices.reshape(sizes), ("pipe", "y", "x", "cfg"))
    seq = ("y", "x")
    return jax.shard_map(
        per_device,
        mesh=grid,
        in_specs=(
            P("cfg", "pipe", seq, None),
            P("pipe", None, None, seq),
            P("pipe", seq, None),
            P("pipe", None, seq),
            P("cfg", "pipe", None, None, seq),
            P("pipe", None, None, None),
            P(),
            P(),
            P(),
            P(),
        ),
        out_specs=(
            P("cfg", "pipe", seq, None),
            P("cfg", "pipe", None, None, seq),
            P("pipe", seq, "cfg"),
        ),
        check_vma=False,
    )
```

time: 540 us -> 417 us (0.77)
  matrix products: 112 us -> 34 us
  blocking collectives: 72.4 us -> 0 us
  Pallas kernels: 0 us -> 30.7 us
  local copies, waits for them, and re-layouts: 50.4 us -> 24.8 us
  waiting for transfers between devices: 262 us -> 287 us
  other arithmetic: 24.3 us -> 12.9 us
  starting transfers between devices: 1.73 us -> 11.3 us
    psum x1 -> x0, blocking collectives: 72.4 us -> none  [per_device(): lax.psum((jnp.sum(jnp.square(queries), axis=-1), jnp.sum(jnp.square(key_c...]
    sub x4 -> x0, matrix products: 41.1 us -> none  [attend(): expo = jnp.exp(scores - top)]
    dot_general x6 -> x2, matrix products: 69 us -> 31.9 us  [the longest x1 20.6 us: per_device(): jnp.dot(gathered, in_weight, preferred_element_type=jnp.float32)]
    pallas_call x0 -> x2, Pallas kernels: none -> 30.7 us  [the longest x1 26.4 us: attend(): pl.pallas_call(attend_body, grid_spec=pltpu.PrefetchScalarGridSpec(num_sc...]
    all_gather x1, waiting for transfers between devices: 115 us -> 124 us  [per_device(): gathered = lax.all_gather(normed, ('y', 'x'), axis=0, tiled=True)]
    dynamic_update_slice x10 -> x0, local copies, waits for them, and re-layouts: 9.79 us -> none  [the longest x2 6.36 us: per_device(): lax.dynamic_update_slice(stale_kv[0, 0, 1], value_normed, (first_row, jnp...]
    ppermute x1 -> x5, starting transfers between devices: 0.09 us -> 9.66 us  [partner_2(): lax.ppermute(shard, axis, [(i, i ^ stride) for i in range(lax.axis_size(a...]
    ppermute x1 -> x5, waiting for transfers between devices: 0.01 us -> 7.68 us  [partner_2(): lax.ppermute(shard, axis, [(i, i ^ stride) for i in range(lax.axis_size(a...]
  transfers between devices with their start and end apart: 4 -> 8, of which waited for: 3 -> 8; matrix products, arithmetic and copies ran while one was open for 6% -> 4% of each run, Pallas kernels for 0% -> 0%
where the time goes in v1:
time: 417 us; the launch traced here: 416 us
  waiting for transfers between devices  287 us (69%)
  matrix products  34 us (8%)
  Pallas kernels  30.7 us (7%)
  local copies, waits for them, and re-layouts  24.8 us (6%)
  between operations  15.6 us (4%)
  other arithmetic  12.9 us (3%)
  starting transfers between devices  11.3 us (3%)
    reduce_scatter x1, waiting for transfers between devices, per_device(): lax.psum_scatter(jnp.dot(attended, out_weight[0], preferred_element_type=...  131 us
    all_gather x1, waiting for transfers between devices, per_device(): gathered = lax.all_gather(normed, ('y', 'x'), axis=0, tiled=True)  124 us
    pallas_call x1, Pallas kernels, attend(): pl.pallas_call(attend_body, grid_spec=pltpu.PrefetchScalarGridSpec(num_sc...  26.4 us
    ppermute x1, waiting for transfers between devices, passed_along(): return lax.ppermute(block, axis, route)  23.8 us
    dot_general x1, matrix products, per_device(): jnp.dot(gathered, in_weight, preferred_element_type=jnp.float32)  20.6 us
    unnamed x11, local copies, waits for them, and re-layouts  18.4 us
    dot_general x1, matrix products, per_device(): jnp.dot(attended, out_weight[0], preferred_element_type=jnp.float32)  11.3 us
    ppermute x5, starting transfers between devices, partner_2(): lax.ppermute(shard, axis, [(i, i ^ stride) for i in range(lax.axis_size(a...  9.66 us
  transfers between devices with their start and end apart: 8, of which 8 were waited for; matrix products, arithmetic and copies ran while one was open for 4% of the time, Pallas kernels for 0%

profile of v1, /device:TPU:0, one launch (start us, length us, event | category | flops | bytes accessed | tf_op | source)
XLA Modules:
  0.0 416.2 jit_solution(14573936038748896562)
XLA Ops:
  8.0 2.4 copy.24
  10.5 4.0 copy.17.mod_ref
  14.5 4.3 %shard_map.121 = bf16[128,5120]{1,0:T(8,128)(2,1)} custom-call(s32[1]{0:T(128)} %copy.27.step_ref, bf16[128,5120]{1,0:T(8,128)(2,1)} %bitcast.40, f32[50,3,5120]{2,1,0:T(4,128)} %copy.17.mod_ref), custom_call_target="tpu_custom_call" | custom-call | tf_op jit(solution)/shard_map/pallas_call | solution.py:52
  18.8 10.8 %copy.18 = bf16[1,5120,3,256]{1,3,2,0:T(8,128)(2,1)} copy(bf16[1,5120,3,256]{3,1,2,0:T(8,128)(2,1)} %param.11) | data formatting | bytes 15728640 | tf_op args[1]
  29.6 124.4 %all-gather.2.cloned.1.call-done = bf16[2048,5120]{1,0:T(8,128)(2,1)} async-done(((bf16[128,5120]{1,0:T(8,128)(2,1)}), bf16[2048,5120]{1,0:T(8,128)(2,1)}) %all-gather.2.cloned.1.call-update) | async-done | bytes 20971536 | tf_op jit(solution)/shard_map/all_gather | solution.py:132
  154.0 20.6 %fusion.20 = f32[2048,768]{1,0:T(8,128)S(1)} fusion(bf16[2048,5120]{1,0:T(8,128)(2,1)} %all-gather.2.cloned.1.call-done, bf16[5120,768]{0,1:T(8,128)(2,1)} %bitcast.39), kind=kOutput, calls=%fused_computation.39 | convolution fusion | flops 16106127360 | bytes 35127296 | tf_op jit(solution)/shard_map/dot_general | solution.py:133
  174.6 2.7 copy-done.1
  179.5 2.3 collective-permute-done
  181.8 3.1 collective-permute-start.1
  184.9 2.3 collective-permute-done.1
  187.1 1.5 collective-permute-start.2
  189.4 1.6 collective-permute-done.2
  191.0 3.4 collective-permute-start.3
  194.4 1.7 fusion.10
  196.5 3.3 fusion.9
  199.9 2.3 fusion.16
  202.1 26.4 %shard_map.122 = bf16[2048,256]{1,0:T(8,128)(2,1)} custom-call(s32[1]{0:T(128)S(6)} %sub.26.slot_ref, bf16[2048,256]{1,0:T(8,128)(2,1)} %get-tuple-element.8.q_ref, bf16[2,2048,256]{2,1,0:T(8,128)(2,1)} %get-tuple-element.10.kf.vf, bf16[2,2048,256]{2,1,0:T(8,128)(2,1)} %get-tuple-element.10.kf.vf, bf16[2,4096,256]{2,1,0:T(8,128)(2,1)} %bitcast.54, ...), custom_call_target="tpu_custom_call" | custom-call | flops 8589934592 | bytes 4194304 | tf_op jit(solution)/shard_map/pallas_call | solution.py:89
  228.5 11.3 %convolution_convert_fusion = bf16[2048,5120]{1,0:T(8,128)(2,1)} fusion(bf16[2048,256]{1,0:T(8,128)(2,1)} %shard_map.122, bf16[1,256,5120]{2,1,0:T(8,128)(2,1)S(1)} %copy-done), kind=kOutput, calls=%fused_computation | convolution fusion | flops 5379194880 | bytes 24641536 | tf_op jit(solution)/shard_map/dot_general | solution.py:148
  240.6 131.0 %reduce-scatter.2.cloned.1.call-done = bf16[128,5120]{1,0:T(8,128)(2,1)} async-done(((bf16[2048,5120]{1,0:T(8,128)(2,1)}), bf16[128,5120]{1,0:T(8,128)(2,1)}) %reduce-scatter.2.cloned.1.call-update) | async-done | bytes 1310736 | tf_op jit(solution)/shard_map/reduce_scatter | solution.py:147
  371.6 3.3 convert_reduce_fusion
  377.3 1.8 fusion.2
  379.1 2.1 fusion.19
  383.1 23.8 %collective-permute-done.4 = bf16[128,5120]{1,0:T(8,128)(2,1)} collective-permute-done((bf16[128,5120]{1,0:T(8,128)(2,1)}, bf16[128,5120]{1,0:T(8,128)(2,1)}, u32[]{:S(2)}, u32[]{:S(2)}) %collective-permute-start.4) | collective-permute-done | bytes 1310752 | tf_op jit(solution)/shard_map/ppermute | solution.py:22
  407.0 2.5 copy.28
  (29 shorter events, 7.8 us)
Async XLA Ops:
  7.2 221.4 %copy-start = (bf16[1,256,5120]{2,1,0:T(8,128)(2,1)S(1)}, bf16[1,256,5120]{2,1,0:T(8,128)(2,1)}, u32[]{:S(2)}) copy-start(bf16[1,256,5120]{2,1,0:T(8,128)(2,1)} %param.12) | copy-start | bytes 7864324
  7.2 146.8 %all-gather.2.cloned.1.call-start = ((), (), s32[]{:S(2)}) async-start(), calls=%async_computation.1 | async-start | bytes 22282240 | tf_op jit(solution)/shard_map/all_gather | solution.py:132
  18.8 352.8 %reduce-scatter.2.cloned.1.call-start = ((), (), s32[]{:S(2)}) async-start(), calls=%async_computation.2 | async-start | bytes 22282240 | tf_op jit(solution)/shard_map/reduce_scatter | solution.py:147
  174.6 2.7 copy-start.1
  177.3 11.4 %copy-start.2 = (f32[1,2,256]{2,1,0:T(2,128)S(1)}, f32[1,2,256]{2,1,0:T(2,128)}, u32[]{:S(2)}) copy-start(f32[1,2,256]{2,1,0:T(2,128)} %param.13) | copy-start | bytes 6148
  178.0 3.8 collective-permute-start
  181.8 5.3 %collective-permute-start.1 = (f32[2,2048]{1,0:T(2,128)S(1)}, f32[2,2048]{1,0:T(2,128)S(1)}, u32[]{:S(2)}, u32[]{:S(2)}) collective-permute-start(f32[2,2048]{1,0:T(2,128)S(1)} %fusion.15), channel_id=1, source_target_pairs={{0,4},{2,6},{4,0},{6,2},{1,5},{3,7},{5,1},{7,3},{8,12},{10,14},{12... | collective-permute-start | bytes 49160 | tf_op jit(solution)/shard_map/ppermute | solution.py:26
  187.1 3.8 collective-permute-start.2
  191.0 5.5 %collective-permute-start.3 = (f32[2,2048]{1,0:T(2,128)S(1)}, f32[2,2048]{1,0:T(2,128)S(1)}, u32[]{:S(2)}, u32[]{:S(2)}) collective-permute-start(f32[2,2048]{1,0:T(2,128)S(1)} %add.78), channel_id=1, source_target_pairs={{0,16},{8,24},{16,0},{24,8},{1,17},{9,25},{17,1},{25,9},{2,18},{10... | collective-permute-start | bytes 49160 | tf_op jit(solution)/shard_map/ppermute | solution.py:26
  371.6 7.6 %copy-start.3 = (bf16[5120,64]{0,1:T(8,128)(2,1)S(1)}, bf16[5120,64]{0,1:T(8,128)(2,1)}, u32[]{:S(2)}) copy-start(bf16[5120,64]{0,1:T(8,128)(2,1)} %param.17) | copy-start | bytes 1966084
  374.9 32.1 %collective-permute-start.4 = (bf16[128,5120]{1,0:T(8,128)(2,1)}, bf16[128,5120]{1,0:T(8,128)(2,1)}, u32[]{:S(2)}, u32[]{:S(2)}) collective-permute-start(bf16[128,5120]{1,0:T(8,128)(2,1)} %get-tuple-element.6), channel_id=1, source_target_pairs={{96,0},{0,32},{32,64},{64,96},{97,1},{1,33},{33,65},{65,97},{98,2}... | collective-permute-start | bytes 3932168 | tf_op jit(solution)/shard_map/ppermute | solution.py:22
  381.2 1.3 collective-permute-start.5
Sparse Core Ops, SparseCore 0:
  18.9 135.0 all-gather.1
  240.0 131.5 reduce-scatter.1

commit v2 on v1

--- a/solution.py
+++ b/solution.py
@@ -40,32 +40,27 @@
     return (values - center) * lax.rsqrt(spread + epsilon) * (1.0 + scale_row) + shift_row
 
 
-def norm_body(step_ref, x_ref, mod_ref, out_ref):
-    out_ref[...] = modulate(x_ref[...], mod_ref[0, 0:1, :], mod_ref[0, 1:2, :]).astype(
-        jnp.bfloat16
-    )
-
-
-def norm_rows(timestep, tokens, table):
+def norm_body(x_ref, mod_ref, out_ref):
+    out_ref[...] = modulate(x_ref[...], mod_ref[0:1, :], mod_ref[1:2, :]).astype(jnp.bfloat16)
+
+
+def norm_rows(tokens, table):
     rows, width = tokens.shape
     part = rows // 4
     return pl.pallas_call(
         norm_body,
-        grid_spec=pltpu.PrefetchScalarGridSpec(
-            num_scalar_prefetch=1,
-            grid=(4,),
-            in_specs=[
-                pl.BlockSpec((part, width), lambda i, t: (i, 0)),
-                pl.BlockSpec((1,) + table.shape[1:], lambda i, t: (t[0], 0, 0)),
-            ],
-            out_specs=pl.BlockSpec((part, width), lambda i, t: (i, 0)),
-        ),
+        grid=(4,),
+        in_specs=[
+            pl.BlockSpec((part, width), lambda i: (i, 0)),
+            pl.BlockSpec(table.shape, lambda i: (0, 0)),
+        ],
+        out_specs=pl.BlockSpec((part, width), lambda i: (i, 0)),
         out_shape=jax.ShapeDtypeStruct((rows, width), jnp.bfloat16),
-    )(timestep, tokens, table)
-
-
-def attend_body(slot_ref, q_ref, kf, vf, ks, vs, out_ref):
-    queries = q_ref[...]
+    )(tokens, table)
+
+
+def attend_body(where_ref, q_ref, kf, vf, ks, vs, out_ref):
+    queries = q_ref[...].reshape(out_ref.shape)
     top = total = mixed = None
     for keys, values in ((kf, vf), (ks, vs)):
         scores = lax.dot_general(queries, keys[0], LAST, preferred_element_type=jnp.float32)
@@ -83,22 +78,24 @@
     out_ref[...] = (mixed / total).astype(jnp.bfloat16)
 
 
-def attend(other_slot, queries, fresh, stale, block):
-    rows, width = queries.shape
+def attend(where, queries, fresh, stale):
+    groups, columns, width = queries.shape
+    part = columns // lax.axis_size("x")
+    rows = groups * part
     keys = fresh.shape[1]
     return pl.pallas_call(
         attend_body,
         grid_spec=pltpu.PrefetchScalarGridSpec(
             num_scalar_prefetch=1,
-            grid=(width // HEAD, rows // block),
+            grid=(width // HEAD,),
             in_specs=[
-                pl.BlockSpec((block, HEAD), lambda h, i, s: (i, h)),
-                pl.BlockSpec((1, keys, HEAD), lambda h, i, s: (0, 0, h)),
-                pl.BlockSpec((1, keys, HEAD), lambda h, i, s: (1, 0, h)),
-                pl.BlockSpec((1, keys, HEAD), lambda h, i, s: (0, s[0], h)),
-                pl.BlockSpec((1, keys, HEAD), lambda h, i, s: (1, s[0], h)),
+                pl.BlockSpec((groups, part, HEAD), lambda h, w: (0, w[1], h)),
+                pl.BlockSpec((1, keys, HEAD), lambda h, w: (0, 0, h)),
+                pl.BlockSpec((1, keys, HEAD), lambda h, w: (1, 0, h)),
+                pl.BlockSpec((1, keys, HEAD), lambda h, w: (0, w[0], h)),
+                pl.BlockSpec((1, keys, HEAD), lambda h, w: (1, w[0], h)),
             ],
-            out_specs=pl.BlockSpec((block, HEAD), lambda h, i, s: (i, h)),
+            out_specs=pl.BlockSpec((rows, HEAD), lambda h, w: (0, h)),
         ),
         out_shape=jax.ShapeDtypeStruct((rows, width), jnp.bfloat16),
         compiler_params=pltpu.CompilerParams(vmem_limit_bytes=56 * 2**20),
@@ -107,7 +104,53 @@
             bytes_accessed=8 * keys * width,
             transcendentals=4 * rows * keys,
         ),
-    )(other_slot, queries, fresh, fresh, stale, stale)
+    )(where, queries, fresh, fresh, stale, stale)
+
+
+def project_body(where_ref, *refs):
+    count = (len(refs) - 1) // 4
+    left = jnp.concatenate([ref[...] for ref in refs[: 2 * count]], axis=1)
+    right = jnp.concatenate([ref[0] for ref in refs[2 * count : -1]], axis=0)
+    refs[-1][...] = jnp.dot(left, right, preferred_element_type=jnp.float32).astype(jnp.bfloat16)
+
+
+def project(where, shares, own, other, block):
+    count = len(shares)
+    rows = shares[0].shape[0] // lax.axis_size("y")
+    half = own.shape[1]
+    width = own.shape[2]
+    left_specs = []
+    right_specs = []
+    for j in range(count):
+        left_specs += [
+            pl.BlockSpec((rows, half), lambda i, w: (w[0], w[1])),
+            pl.BlockSpec((rows, half), lambda i, w: (w[0], 1 - w[1])),
+        ]
+        right_specs += [
+            pl.BlockSpec((1, half, block), lambda i, w, j=j: (w[2 + j], 0, i)),
+            pl.BlockSpec((1, half, block), lambda i, w, j=j: (w[2 + j], 0, i)),
+        ]
+    lefts = [share for share in shares for _ in range(2)]
+    return pl.pallas_call(
+        project_body,
+        grid_spec=pltpu.PrefetchScalarGridSpec(
+            num_scalar_prefetch=1,
+            grid=(width // block,),
+            in_specs=left_specs + right_specs,
+            out_specs=pl.BlockSpec((rows, block), lambda i, w: (0, i)),
+        ),
+        out_shape=jax.ShapeDtypeStruct((rows, width), jnp.bfloat16),
+        compiler_params=pltpu.CompilerParams(vmem_limit_bytes=56 * 2**20),
+        cost_estimate=pl.CostEstimate(
+            flops=4 * rows * count * half * width,
+            bytes_accessed=4 * count * half * width,
+            transcendentals=0,
+        ),
+    )(where, *lefts, *([own, other] * count))
+
+
+def add_rows(one, two):
+    return (one.astype(jnp.float32) + two.astype(jnp.float32)).astype(jnp.bfloat16)
 
 
 def per_device(
@@ -128,8 +171,15 @@
     model_width = in_weight.shape[0]
     local_width = in_weight.shape[2]
     in_weight = in_weight.reshape(model_width, 3 * local_width)
-    normed = norm_rows(timestep, tokens_in, modulation[0])
+    mod_rows = lax.dynamic_index_in_dim(modulation[0], step_row, 0, keepdims=False)
+    normed = norm_rows(tokens_in, mod_rows)
     gathered = lax.all_gather(normed, ("y", "x"), axis=0, tiled=True)
+    x_index, y_index, core = (lax.axis_index(name) for name in ("x", "y", "cfg"))
+    half = out_weight.shape[1] // 2
+    mine = lax.dynamic_slice_in_dim(out_weight[0], core * half, half, 0)
+    gathered, mine = lax.optimization_barrier((gathered, mine))
+    own_weights = lax.all_gather(mine, "x", axis=0)
+    other_weights = partner_2(own_weights, "cfg", 1)
     projections = jnp.dot(gathered, in_weight, preferred_element_type=jnp.float32)
     queries = projections[:, :local_width]
     key_cols = projections[:, local_width : 2 * local_width]
@@ -143,14 +193,36 @@
     key_normed = (key_cols * scales[1] * qk_gain[0, 1]).astype(jnp.bfloat16)
     fresh_pair = jnp.stack([key_normed, value_cols.astype(jnp.bfloat16)])
     patch_slot = jnp.mod(patch_index - lax.axis_index("pipe"), NPATCH)
-    attended = attend(1 - patch_slot, query_normed, fresh_pair, stale_kv[0, 0], 512)
-    projected = lax.psum_scatter(
-        jnp.dot(attended, out_weight[0], preferred_element_type=jnp.float32).astype(jnp.bfloat16),
-        ("y", "x"),
-        scatter_dimension=0,
-        tiled=True,
-    ).astype(jnp.float32)
-    gate = lax.dynamic_slice(modulation[0], (step_row, 2, 0), (1, 1, model_width))[0]
+    columns, lines = lax.axis_size("x"), lax.axis_size("y")
+    query_groups = query_normed.reshape(lines, -1, local_width)
+    shares = {}
+    for j in (2, 1, 3, 0):
+        where = jnp.concatenate([1 - patch_slot, ((x_index + j) % columns)[None]])
+        block = attend(where, query_groups, fresh_pair, stale_kv[0, 0])
+        shares[j] = passed_along(block, "x", j) if j else block
+    sources = [(x_index - j) % columns for j in range(columns)]
+
+    def rows_for(k):
+        where = jnp.stack([(y_index + k) % lines, core] + sources).astype(jnp.int32)
+        return project(where, [shares[j] for j in range(columns)], own_weights, other_weights, 1024)
+
+    cut = tokens_in.shape[0] // 2
+    across = rows_for(2)
+    from_below = passed_along(across[:cut], "y", 1)
+    from_above = passed_along(across[cut:], "y", 3)
+    up = rows_for(1)
+    low_up = passed_along(up[cut:], "y", 1)
+    down = rows_for(3)
+    high_down = passed_along(down[:cut], "y", 3)
+    high_up = passed_along(add_rows(up[:cut], from_below), "y", 1)
+    low_down = passed_along(add_rows(down[cut:], from_above), "y", 3)
+    projected = rows_for(0).astype(jnp.float32) + jnp.concatenate(
+        [
+            high_up.astype(jnp.float32) + high_down.astype(jnp.float32),
+            low_up.astype(jnp.float32) + low_down.astype(jnp.float32),
+        ]
+    )
+    gate = mod_rows[2:3]
     block_out = (tokens_in.astype(jnp.float32) + gate * projected).astype(jnp.bfloat16)
     forwarded = passed_along(block_out, "pipe", 1)
     head_rows = lax.dynamic_index_in_dim(head_mod, step_row, 0, keepdims=False)

time: 417 us -> 401 us (0.962)
  waiting for transfers between devices: 287 us -> 220 us
  Pallas kernels: 30.7 us -> 71.8 us
  starting transfers between devices: 11.3 us -> 23.4 us
  matrix products: 34 us -> 22.9 us
  local copies, waits for them, and re-layouts: 24.8 us -> 30.4 us
    reduce_scatter x1 -> x0, waiting for transfers between devices: 131 us -> none  [per_device(): lax.psum_scatter(jnp.dot(attended, out_weight[0], preferred_element_type=...]
    all_gather x0 -> x1, waiting for transfers between devices: none -> 47.6 us  [per_device(): own_weights = lax.all_gather(mine, 'x', axis=0)]
    pallas_call x1 -> x5, Pallas kernels: 4.26 us -> 36 us  [the longest x4 31.7 us: project(): pl.pallas_call(project_body, grid_spec=pltpu.PrefetchScalarGridSpec(num_s...]
    ppermute x1 -> x10, starting transfers between devices: 1.54 us -> 15.2 us  [passed_along(): return lax.ppermute(block, axis, route)]
    dot_general x1 -> x0, matrix products: 11.3 us -> none  [per_device(): jnp.dot(attended, out_weight[0], preferred_element_type=jnp.float32)]
    pallas_call x1 -> x4, Pallas kernels: 26.4 us -> 35.8 us  [attend(): pl.pallas_call(attend_body, grid_spec=pltpu.PrefetchScalarGridSpec(num_sc...]
    ppermute x1 -> x10, waiting for transfers between devices: 23.8 us -> 32.3 us  [passed_along(): return lax.ppermute(block, axis, route)]
    all_gather x1, waiting for transfers between devices: 124 us -> 133 us  [per_device(): gathered = lax.all_gather(normed, ('y', 'x'), axis=0, tiled=True)]
  transfers between devices with their start and end apart: 8 -> 18, of which waited for: 8 -> 11; matrix products, arithmetic and copies ran while one was open for 4% -> 14% of each run, Pallas kernels for 0% -> 15%
where the time goes in v2:
time: 401 us; the launch traced here: 400 us
  waiting for transfers between devices  220 us (55%)
  Pallas kernels  71.8 us (18%)
  local copies, waits for them, and re-layouts  30.4 us (8%)
  starting transfers between devices  23.4 us (6%)
  matrix products  22.9 us (6%)
  between operations  15.8 us (4%)
  other arithmetic  15.5 us (4%)
    all_gather x1, waiting for transfers between devices, per_device(): gathered = lax.all_gather(normed, ('y', 'x'), axis=0, tiled=True)  133 us
    all_gather x1, waiting for transfers between devices, per_device(): own_weights = lax.all_gather(mine, 'x', axis=0)  47.6 us
    pallas_call x4, Pallas kernels, attend(): pl.pallas_call(attend_body, grid_spec=pltpu.PrefetchScalarGridSpec(num_sc...  35.8 us
    ppermute x10, waiting for transfers between devices, passed_along(): return lax.ppermute(block, axis, route)  32.3 us
    pallas_call x4, Pallas kernels, project(): pl.pallas_call(project_body, grid_spec=pltpu.PrefetchScalarGridSpec(num_s...  31.7 us
    dot_general x1, matrix products, per_device(): jnp.dot(gathered, in_weight, preferred_element_type=jnp.float32)  20.8 us
    unnamed x29, local copies, waits for them, and re-layouts  18.3 us
    ppermute x10, starting transfers between devices, passed_along(): return lax.ppermute(block, axis, route)  15.2 us
  transfers between devices with their start and end apart: 18, of which 11 were waited for; matrix products, arithmetic and copies ran while one was open for 14% of the time, Pallas kernels for 15%

profile of v2, /device:TPU:0, one launch (start us, length us, event | category | flops | bytes accessed | tf_op | source)
XLA Modules:
  0.0 399.7 jit_solution(16937197743433126393)
XLA Ops:
  9.7 4.3 %shard_map.121 = bf16[128,5120]{1,0:T(8,128)(2,1)} custom-call(bf16[128,5120]{1,0:T(8,128)(2,1)} %bitcast.80, f32[3,5120]{1,0:T(4,128)} %bitcast.81), custom_call_target="tpu_custom_call" | custom-call | tf_op jit(solution)/shard_map/pallas_call | solution.py:50
  14.1 2.5 dynamic-slice_bitcast_fusion
  16.5 132.7 %all-gather.4.cloned.1.call-done = bf16[2048,5120]{1,0:T(8,128)(2,1)} async-done(((bf16[128,5120]{1,0:T(8,128)(2,1)}), bf16[2048,5120]{1,0:T(8,128)(2,1)}) %all-gather.4.cloned.1.call-update) | async-done | bytes 20971536 | tf_op jit(solution)/shard_map/all_gather | solution.py:176
  149.9 10.7 %copy.13 = bf16[1,5120,3,256]{1,3,2,0:T(8,128)(2,1)} copy(bf16[1,5120,3,256]{3,1,2,0:T(8,128)(2,1)} %param.11) | data formatting | bytes 15728640 | tf_op args[1]
  160.6 47.6 %all-gather.6.cloned.1.call-done = bf16[512,5120]{1,0:T(8,128)(2,1)} async-done(((bf16[128,5120]{1,0:T(8,128)(2,1)}), bf16[512,5120]{1,0:T(8,128)(2,1)}) %all-gather.6.cloned.1.call-update) | async-done | bytes 5242896 | tf_op jit(solution)/shard_map/all_gather | solution.py:181
  208.2 20.8 %fusion.24 = f32[2048,768]{1,0:T(8,128)S(1)} fusion(bf16[2048,5120]{1,0:T(8,128)(2,1)} %all-gather.4.cloned.1.call-done, bf16[5120,768]{0,1:T(8,128)(2,1)} %bitcast.79), kind=kOutput, calls=%fused_computation.51 | convolution fusion | flops 16106127360 | bytes 35127296 | tf_op jit(solution)/shard_map/dot_general | solution.py:183
  229.1 2.6 copy-done.4
  239.1 2.4 collective-permute-done.1
  245.3 3.1 collective-permute-start.3
  250.7 3.3 fusion.11
  256.3 8.9 %shard_map.125 = bf16[512,256]{1,0:T(8,128)(2,1)} custom-call(s32[2]{0:T(128)} %pad_add_fusion.3.where_ref, bf16[4,512,256]{2,1,0:T(8,128)(2,1)} %bitcast.75, bf16[2,2048,256]{2,1,0:T(8,128)(2,1)} %get-tuple-element.14.kf.vf, bf16[2,2048,256]{2,1,0:T(8,128)(2,1)} %get-tuple-element.14.kf.vf, bf16[2,4096,256]{2,1,0:T(8,128)(2,1)} %bitcast.67, ...), custom_call_target="tpu_custom_call" | custom-call | flops 2147483648 | bytes 4194304 | tf_op jit(solution)/shard_map/pallas_call | solution.py:86
  266.3 8.9 %shard_map.124 = bf16[512,256]{1,0:T(8,128)(2,1)} custom-call(s32[2]{0:T(128)} %pad_add_fusion.2.where_ref, bf16[4,512,256]{2,1,0:T(8,128)(2,1)} %bitcast.76, bf16[2,2048,256]{2,1,0:T(8,128)(2,1)} %get-tuple-element.14.kf.vf, bf16[2,2048,256]{2,1,0:T(8,128)(2,1)} %get-tuple-element.14.kf.vf, bf16[2,4096,256]{2,1,0:T(8,128)(2,1)} %bitcast.69, ...), custom_call_target="tpu_custom_call" | custom-call | flops 2147483648 | bytes 4194304 | tf_op jit(solution)/shard_map/pallas_call | solution.py:86
  277.3 8.9 %shard_map.123 = bf16[512,256]{1,0:T(8,128)(2,1)} custom-call(s32[2]{0:T(128)} %pad_add_fusion.1.where_ref, bf16[4,512,256]{2,1,0:T(8,128)(2,1)} %bitcast.77, bf16[2,2048,256]{2,1,0:T(8,128)(2,1)} %get-tuple-element.14.kf.vf, bf16[2,2048,256]{2,1,0:T(8,128)(2,1)} %get-tuple-element.14.kf.vf, bf16[2,4096,256]{2,1,0:T(8,128)(2,1)} %bitcast.71, ...), custom_call_target="tpu_custom_call" | custom-call | flops 2147483648 | bytes 4194304 | tf_op jit(solution)/shard_map/pallas_call | solution.py:86
  287.4 8.9 %shard_map.122.refs_0_.refs_1_ = bf16[512,256]{1,0:T(8,128)(2,1)} custom-call(s32[2]{0:T(128)} %pad_add_fusion.where_ref, bf16[4,512,256]{2,1,0:T(8,128)(2,1)} %bitcast.78, bf16[2,2048,256]{2,1,0:T(8,128)(2,1)} %get-tuple-element.14.kf.vf, bf16[2,2048,256]{2,1,0:T(8,128)(2,1)} %get-tuple-element.14.kf.vf, bf16[2,4096,256]{2,1,0:T(8,128)(2,1)} %bitcast.73, ...), custom_call_target="tpu_custom_call" | custom-call | flops 2147483648 | bytes 4194304 | tf_op jit(solution)/shard_map/pallas_call | solution.py:86
  297.2 7.9 %shard_map.128 = bf16[128,5120]{1,0:T(8,128)(2,1)} custom-call(s32[6]{0:T(128)} %stack.88.where_ref, bf16[512,256]{1,0:T(8,128)(2,1)} %shard_map.122.refs_0_.refs_1_, bf16[512,256]{1,0:T(8,128)(2,1)} %shard_map.122.refs_0_.refs_1_, bf16[512,256]{1,0:T(8,128)(2,1)} %copy-done.3, bf16[512,256]{1,0:T(8,128)(2,1)} %copy-done.3, bf16[512,256]{1,0:T(8,128)(2,1)} %copy-done.2, ...), custom_call_target="tpu_custom_call" | custom-call | flops 1342177280 | bytes 10485760 | tf_op jit(solution)/shard_map/pallas_call | solution.py:134
  305.2 2.4 fusion.20
  311.6 7.9 %shard_map.129 = bf16[128,5120]{1,0:T(8,128)(2,1)} custom-call(s32[6]{0:T(128)} %stack.90.where_ref, bf16[512,256]{1,0:T(8,128)(2,1)} %shard_map.122.refs_0_.refs_1_, bf16[512,256]{1,0:T(8,128)(2,1)} %shard_map.122.refs_0_.refs_1_, bf16[512,256]{1,0:T(8,128)(2,1)} %copy-done.3, bf16[512,256]{1,0:T(8,128)(2,1)} %copy-done.3, bf16[512,256]{1,0:T(8,128)(2,1)} %copy-done.2, ...), custom_call_target="tpu_custom_call" | custom-call | flops 1342177280 | bytes 10485760 | tf_op jit(solution)/shard_map/pallas_call | solution.py:134
  322.7 8.0 %shard_map.127 = bf16[128,5120]{1,0:T(8,128)(2,1)} custom-call(s32[6]{0:T(128)} %stack.86.where_ref, bf16[512,256]{1,0:T(8,128)(2,1)} %shard_map.122.refs_0_.refs_1_, bf16[512,256]{1,0:T(8,128)(2,1)} %shard_map.122.refs_0_.refs_1_, bf16[512,256]{1,0:T(8,128)(2,1)} %copy-done.3, bf16[512,256]{1,0:T(8,128)(2,1)} %copy-done.3, bf16[512,256]{1,0:T(8,128)(2,1)} %copy-done.2, ...), custom_call_target="tpu_custom_call" | custom-call | flops 1342177280 | bytes 10485760 | tf_op jit(solution)/shard_map/pallas_call | solution.py:134
  332.2 3.0 collective-permute-start.12
  335.1 8.0 %shard_map.126 = bf16[128,5120]{1,0:T(8,128)(2,1)} custom-call(s32[6]{0:T(128)} %stack.78.where_ref, bf16[512,256]{1,0:T(8,128)(2,1)} %shard_map.122.refs_0_.refs_1_, bf16[512,256]{1,0:T(8,128)(2,1)} %shard_map.122.refs_0_.refs_1_, bf16[512,256]{1,0:T(8,128)(2,1)} %copy-done.3, bf16[512,256]{1,0:T(8,128)(2,1)} %copy-done.3, bf16[512,256]{1,0:T(8,128)(2,1)} %copy-done.2, ...), custom_call_target="tpu_custom_call" | custom-call | flops 1342177280 | bytes 10485760 | tf_op jit(solution)/shard_map/pallas_call | solution.py:134
  347.0 3.0 collective-permute-start.13
  350.0 8.6 %collective-permute-done.9 = bf16[64,5120]{1,0:T(8,128)(2,1)S(1)} collective-permute-done((bf16[64,5120]{1,0:T(8,128)(2,1)S(1)}, bf16[64,5120]{1,0:T(8,128)(2,1)S(1)}, u32[]{:S(2)}, u32[]{:S(2)}) %collective-permute-start.9) | collective-permute-done | bytes 655392 | tf_op jit(solution)/shard_map/ppermute | solution.py:22
  370.6 19.8 %collective-permute-done.14 = bf16[128,5120]{1,0:T(8,128)(2,1)} collective-permute-done((bf16[128,5120]{1,0:T(8,128)(2,1)}, bf16[128,5120]{1,0:T(8,128)(2,1)}, u32[]{:S(2)}, u32[]{:S(2)}) %collective-permute-start.14) | collective-permute-done | bytes 1310752 | tf_op jit(solution)/shard_map/ppermute | solution.py:22
  390.4 2.5 copy.20
  (89 shorter events, 47.1 us)
Async XLA Ops:
  7.2 142.0 %all-gather.4.cloned.1.call-start = ((), (), s32[]{:S(2)}) async-start(), calls=%async_computation | async-start | bytes 22282240 | tf_op jit(solution)/shard_map/all_gather | solution.py:176
  14.0 194.2 %all-gather.6.cloned.1.call-start = ((), (), s32[]{:S(2)}) async-start(), calls=%async_computation.1 | async-start | bytes 6553600 | tf_op jit(solution)/shard_map/all_gather | solution.py:181
  149.9 10.7 %copy-start.11 = (f32[1,2,256]{2,1,0:T(2,128)S(1)}, f32[1,2,256]{2,1,0:T(2,128)}, u32[]{:S(2)}) copy-start(f32[1,2,256]{2,1,0:T(2,128)} %param.13) | copy-start | bytes 6148
  208.2 88.2 %collective-permute-start.7 = (bf16[4,128,5120]{2,1,0:T(8,128)(2,1)}, bf16[4,128,5120]{2,1,0:T(8,128)(2,1)}, u32[]{:S(2)}, u32[]{:S(2)}) collective-permute-start(bf16[4,128,5120]{2,1,0:T(8,128)(2,1)} %bitcast.50), channel_id=1, source_target_pairs={{0,1},{1,0},{2,3},{3,2},{4,5},{5,4},{6,7},{7,6},{8,9},{9,8},{10,11... | collective-permute-start | bytes 15728648 | tf_op jit(solution)/shard_map/ppermute | solution.py:26
  232.3 3.8 collective-permute-start
  236.2 5.3 %collective-permute-start.1 = (f32[2,2048]{1,0:T(2,128)S(1)}, f32[2,2048]{1,0:T(2,128)S(1)}, u32[]{:S(2)}, u32[]{:S(2)}) collective-permute-start(f32[2,2048]{1,0:T(2,128)S(1)} %fusion.17), channel_id=1, source_target_pairs={{0,4},{2,6},{4,0},{6,2},{1,5},{3,7},{5,1},{7,3},{8,12},{10,14},{12... | collective-permute-start | bytes 49160 | tf_op jit(solution)/shard_map/ppermute | solution.py:26
  241.5 3.8 collective-permute-start.2
  245.3 5.3 %collective-permute-start.3 = (f32[2,2048]{1,0:T(2,128)S(1)}, f32[2,2048]{1,0:T(2,128)S(1)}, u32[]{:S(2)}, u32[]{:S(2)}) collective-permute-start(f32[2,2048]{1,0:T(2,128)S(1)} %add.157), channel_id=1, source_target_pairs={{0,16},{8,24},{16,0},{24,8},{1,17},{9,25},{17,1},{25,9},{2,18},{10... | collective-permute-start | bytes 49160 | tf_op jit(solution)/shard_map/ppermute | solution.py:26
  265.3 31.1 %collective-permute-start.6 = (bf16[512,256]{1,0:T(8,128)(2,1)}, bf16[512,256]{1,0:T(8,128)(2,1)S(1)}, u32[]{:S(2)}, u32[]{:S(2)}) collective-permute-start(bf16[512,256]{1,0:T(8,128)(2,1)} %shard_map.125), channel_id=1, source_target_pairs={{2,0},{4,2},{6,4},{0,6},{3,1},{5,3},{7,5},{1,7},{10,8},{12,10},{14... | collective-permute-start | bytes 786440 | tf_op jit(solution)/shard_map/ppermute | solution.py:22
  275.3 21.1 %collective-permute-start.5 = (bf16[512,256]{1,0:T(8,128)(2,1)}, bf16[512,256]{1,0:T(8,128)(2,1)S(1)}, u32[]{:S(2)}, u32[]{:S(2)}) collective-permute-start(bf16[512,256]{1,0:T(8,128)(2,1)} %shard_map.124), channel_id=1, source_target_pairs={{4,0},{6,2},{0,4},{2,6},{5,1},{7,3},{1,5},{3,7},{12,8},{14,10},{8,... | collective-permute-start | bytes 786440 | tf_op jit(solution)/shard_map/ppermute | solution.py:22
  286.2 10.1 %collective-permute-start.4 = (bf16[512,256]{1,0:T(8,128)(2,1)}, bf16[512,256]{1,0:T(8,128)(2,1)S(1)}, u32[]{:S(2)}, u32[]{:S(2)}) collective-permute-start(bf16[512,256]{1,0:T(8,128)(2,1)} %shard_map.123), channel_id=1, source_target_pairs={{6,0},{0,2},{2,4},{4,6},{7,1},{1,3},{3,5},{5,7},{14,8},{8,10},{10,... | collective-permute-start | bytes 786440 | tf_op jit(solution)/shard_map/ppermute | solution.py:22
  307.6 35.5 %collective-permute-start.8 = (bf16[64,5120]{1,0:T(8,128)(2,1)}, bf16[64,5120]{1,0:T(8,128)(2,1)}, u32[]{:S(2)}, u32[]{:S(2)}) collective-permute-start(bf16[64,5120]{1,0:T(8,128)(2,1)} %get-tuple-element.17), channel_id=1, source_target_pairs={{24,0},{0,8},{8,16},{16,24},{25,1},{1,9},{9,17},{17,25},{26,2},{2,... | collective-permute-start | bytes 1966088 | tf_op jit(solution)/shard_map/ppermute | solution.py:22
  320.7 11.5 %copy-start.9 = (bf16[64,5120]{1,0:T(8,128)(2,1)S(1)}, bf16[64,5120]{1,0:T(8,128)(2,1)}, u32[]{:S(2)}) copy-start(bf16[64,5120]{1,0:T(8,128)(2,1)} %get-tuple-element.18) | copy-start | bytes 1966084
  320.7 29.3 %collective-permute-start.10 = (bf16[64,5120]{1,0:T(8,128)(2,1)S(1)}, bf16[64,5120]{1,0:T(8,128)(2,1)S(1)}, u32[]{:S(2)}, u32[]{:S(2)}) collective-permute-start(bf16[64,5120]{1,0:T(8,128)(2,1)S(1)} %slice.77), channel_id=1, source_target_pairs={{8,0},{16,8},{24,16},{0,24},{9,1},{17,9},{25,17},{1,25},{10,2},{18... | collective-permute-start | bytes 1966088 | tf_op jit(solution)/shard_map/ppermute | solution.py:22
  331.8 26.9 %collective-permute-start.11 = (bf16[64,5120]{1,0:T(8,128)(2,1)S(1)}, bf16[64,5120]{1,0:T(8,128)(2,1)S(1)}, u32[]{:S(2)}, u32[]{:S(2)}) collective-permute-start(bf16[64,5120]{1,0:T(8,128)(2,1)S(1)} %slice.78), channel_id=1, source_target_pairs={{24,0},{0,8},{8,16},{16,24},{25,1},{1,9},{9,17},{17,25},{26,2},{2,... | collective-permute-start | bytes 1966088 | tf_op jit(solution)/shard_map/ppermute | solution.py:22
  332.2 11.0 %copy-start.7 = (bf16[128,5120]{1,0:T(8,128)(2,1)S(1)}, bf16[128,5120]{1,0:T(8,128)(2,1)}, u32[]{:S(2)}) copy-start(bf16[128,5120]{1,0:T(8,128)(2,1)} %shard_map.127) | copy-start | bytes 3932164
  332.2 14.6 %collective-permute-start.12 = (bf16[64,5120]{1,0:T(8,128)(2,1)S(1)}, bf16[64,5120]{1,0:T(8,128)(2,1)S(1)}, u32[]{:S(2)}, u32[]{:S(2)}) collective-permute-start(bf16[64,5120]{1,0:T(8,128)(2,1)S(1)} %copy-done.9), channel_id=1, source_target_pairs={{8,0},{16,8},{24,16},{0,24},{9,1},{17,9},{25,17},{1,25},{10,2},{18... | collective-permute-start | bytes 1966088 | tf_op jit(solution)/shard_map/ppermute | solution.py:22
  344.5 14.1 %collective-permute-start.9 = (bf16[64,5120]{1,0:T(8,128)(2,1)S(1)}, bf16[64,5120]{1,0:T(8,128)(2,1)S(1)}, u32[]{:S(2)}, u32[]{:S(2)}) collective-permute-start(bf16[64,5120]{1,0:T(8,128)(2,1)S(1)} %add_convert_fusion.1), channel_id=1, source_target_pairs={{24,0},{0,8},{8,16},{16,24},{25,1},{1,9},{9,17},{17,25},{26,2},{2,... | collective-permute-start | bytes 1966088 | tf_op jit(solution)/shard_map/ppermute | solution.py:22
  347.0 13.7 %copy-start.5 = (bf16[128,5120]{1,0:T(8,128)(2,1)S(1)}, bf16[128,5120]{1,0:T(8,128)(2,1)}, u32[]{:S(2)}) copy-start(bf16[128,5120]{1,0:T(8,128)(2,1)} %shard_map.126) | copy-start | bytes 3932164
  347.0 13.7 %copy-start.8 = (bf16[1,1,128,5120]{3,2,1,0:T(8,128)(2,1)S(1)}, bf16[1,1,128,5120]{3,2,1,0:T(8,128)(2,1)}, u32[]{:S(2)}) copy-start(bf16[1,1,128,5120]{3,2,1,0:T(8,128)(2,1)} %param.10) | copy-start | bytes 3932164
  347.0 13.7 %copy-start.10 = (f32[1,1,1,5120]{3,0,2,1:T(1,128)S(1)}, f32[1,1,1,5120]{3,0,2,1:T(1,128)}, u32[]{:S(2)}) copy-start(f32[1,1,1,5120]{3,0,2,1:T(1,128)} %constant_dynamic-slice_fusion) | copy-start | bytes 61444
  347.0 13.5 %collective-permute-start.13 = (bf16[64,5120]{1,0:T(8,128)(2,1)S(1)}, bf16[64,5120]{1,0:T(8,128)(2,1)S(1)}, u32[]{:S(2)}, u32[]{:S(2)}) collective-permute-start(bf16[64,5120]{1,0:T(8,128)(2,1)S(1)} %add_convert_fusion), channel_id=1, source_target_pairs={{8,0},{16,8},{24,16},{0,24},{9,1},{17,9},{25,17},{1,25},{10,2},{18... | collective-permute-start | bytes 1966088 | tf_op jit(solution)/shard_map/ppermute | solution.py:22
  362.3 28.1 %collective-permute-start.14 = (bf16[128,5120]{1,0:T(8,128)(2,1)}, bf16[128,5120]{1,0:T(8,128)(2,1)}, u32[]{:S(2)}, u32[]{:S(2)}) collective-permute-start(bf16[128,5120]{1,0:T(8,128)(2,1)} %get-tuple-element.10), channel_id=1, source_target_pairs={{96,0},{0,32},{32,64},{64,96},{97,1},{1,33},{33,65},{65,97},{98,2}... | collective-permute-start | bytes 3932168 | tf_op jit(solution)/shard_map/ppermute | solution.py:22
  368.7 1.3 collective-permute-start.15
  (7 other events, 16.6 us)
Sparse Core Ops, SparseCore 0:
  14.1 135.0 all-gather.3
  151.5 56.6 all-gather.5

commit v3 on v2

--- a/solution.py
+++ b/solution.py
@@ -107,42 +107,51 @@
     )(where, queries, fresh, fresh, stale, stale)
 
 
-def project_body(where_ref, *refs):
-    count = (len(refs) - 1) // 4
-    left = jnp.concatenate([ref[...] for ref in refs[: 2 * count]], axis=1)
-    right = jnp.concatenate([ref[0] for ref in refs[2 * count : -1]], axis=0)
-    refs[-1][...] = jnp.dot(left, right, preferred_element_type=jnp.float32).astype(jnp.bfloat16)
-
-
-def project(where, shares, own, other, block):
+def project_body(where_ref, *refs, sources, groups):
+    lefts, refs = refs[: 2 * sources * groups], refs[2 * sources * groups :]
+    rights, outs = refs[: 2 * sources], refs[2 * sources :]
+    left = jnp.concatenate(
+        [
+            jnp.concatenate([ref[...] for ref in lefts[g * 2 * sources : (g + 1) * 2 * sources]], 1)
+            for g in range(groups)
+        ],
+        axis=0,
+    )
+    right = jnp.concatenate([ref[0] for ref in rights], axis=0)
+    terms = jnp.dot(left, right, preferred_element_type=jnp.float32).astype(jnp.bfloat16)
+    cut = outs[0].shape[0]
+    for n, out in enumerate(outs):
+        out[...] = terms[n * cut : (n + 1) * cut]
+
+
+def project(where, groups, shares, own, other, block):
     count = len(shares)
     rows = shares[0].shape[0] // lax.axis_size("y")
     half = own.shape[1]
     width = own.shape[2]
     left_specs = []
     right_specs = []
+    for g in range(groups):
+        for _ in range(count):
+            left_specs += [
+                pl.BlockSpec((rows, half), lambda i, w, g=g: (w[1 + count + g], w[0])),
+                pl.BlockSpec((rows, half), lambda i, w, g=g: (w[1 + count + g], 1 - w[0])),
+            ]
     for j in range(count):
-        left_specs += [
-            pl.BlockSpec((rows, half), lambda i, w: (w[0], w[1])),
-            pl.BlockSpec((rows, half), lambda i, w: (w[0], 1 - w[1])),
-        ]
-        right_specs += [
-            pl.BlockSpec((1, half, block), lambda i, w, j=j: (w[2 + j], 0, i)),
-            pl.BlockSpec((1, half, block), lambda i, w, j=j: (w[2 + j], 0, i)),
-        ]
-    lefts = [share for share in shares for _ in range(2)]
+        right_specs += 2 * [pl.BlockSpec((1, half, block), lambda i, w, j=j: (w[1 + j], 0, i))]
+    lefts = [share for share in shares for _ in range(2)] * groups
     return pl.pallas_call(
-        project_body,
+        functools.partial(project_body, sources=count, groups=groups),
         grid_spec=pltpu.PrefetchScalarGridSpec(
             num_scalar_prefetch=1,
             grid=(width // block,),
             in_specs=left_specs + right_specs,
-            out_specs=pl.BlockSpec((rows, block), lambda i, w: (0, i)),
-        ),
-        out_shape=jax.ShapeDtypeStruct((rows, width), jnp.bfloat16),
+            out_specs=[pl.BlockSpec((rows // 2, block), lambda i, w: (0, i))] * (2 * groups),
+        ),
+        out_shape=[jax.ShapeDtypeStruct((rows // 2, width), jnp.bfloat16)] * (2 * groups),
         compiler_params=pltpu.CompilerParams(vmem_limit_bytes=56 * 2**20),
         cost_estimate=pl.CostEstimate(
-            flops=4 * rows * count * half * width,
+            flops=4 * groups * rows * count * half * width,
             bytes_accessed=4 * count * half * width,
             transcendentals=0,
         ),
@@ -179,7 +188,6 @@
     mine = lax.dynamic_slice_in_dim(out_weight[0], core * half, half, 0)
     gathered, mine = lax.optimization_barrier((gathered, mine))
     own_weights = lax.all_gather(mine, "x", axis=0)
-    other_weights = partner_2(own_weights, "cfg", 1)
     projections = jnp.dot(gathered, in_weight, preferred_element_type=jnp.float32)
     queries = projections[:, :local_width]
     key_cols = projections[:, local_width : 2 * local_width]
@@ -199,32 +207,41 @@
     for j in (2, 1, 3, 0):
         where = jnp.concatenate([1 - patch_slot, ((x_index + j) % columns)[None]])
         block = attend(where, query_groups, fresh_pair, stale_kv[0, 0])
+        if j == 2:
+            own_weights = lax.optimization_barrier((own_weights, block))[0]
+            other_weights = partner_2(own_weights, "cfg", 1)
         shares[j] = passed_along(block, "x", j) if j else block
     sources = [(x_index - j) % columns for j in range(columns)]
 
-    def rows_for(k):
-        where = jnp.stack([(y_index + k) % lines, core] + sources).astype(jnp.int32)
-        return project(where, [shares[j] for j in range(columns)], own_weights, other_weights, 1024)
-
-    cut = tokens_in.shape[0] // 2
-    across = rows_for(2)
-    from_below = passed_along(across[:cut], "y", 1)
-    from_above = passed_along(across[cut:], "y", 3)
-    up = rows_for(1)
-    low_up = passed_along(up[cut:], "y", 1)
-    down = rows_for(3)
-    high_down = passed_along(down[:cut], "y", 3)
-    high_up = passed_along(add_rows(up[:cut], from_below), "y", 1)
-    low_down = passed_along(add_rows(down[cut:], from_above), "y", 3)
-    projected = rows_for(0).astype(jnp.float32) + jnp.concatenate(
+    def rows_for(*places):
+        where = [core] + sources + [(y_index + k) % lines for k in places]
+        return project(
+            jnp.stack(where).astype(jnp.int32),
+            len(places),
+            [shares[j] for j in range(columns)],
+            own_weights,
+            other_weights,
+            1024,
+        )
+
+    high_across, low_across = rows_for(2)
+    from_below = passed_along(high_across, "y", 1)
+    from_above = passed_along(low_across, "y", 3)
+    up_high, up_low, down_high, down_low = rows_for(1, 3)
+    low_up = passed_along(up_low, "y", 1)
+    high_down = passed_along(down_high, "y", 3)
+    high_up = passed_along(add_rows(up_high, from_below), "y", 1)
+    low_down = passed_along(add_rows(down_low, from_above), "y", 3)
+    high, low = (part.astype(jnp.float32) for part in rows_for(0))
+    projected = jnp.concatenate(
         [
-            high_up.astype(jnp.float32) + high_down.astype(jnp.float32),
-            low_up.astype(jnp.float32) + low_down.astype(jnp.float32),
+            high + high_up.astype(jnp.float32) + high_down.astype(jnp.float32),
+            low + low_up.astype(jnp.float32) + low_down.astype(jnp.float32),
         ]
     )
     gate = mod_rows[2:3]
     block_out = (tokens_in.astype(jnp.float32) + gate * projected).astype(jnp.bfloat16)
-    forwarded = passed_along(block_out, "pipe", 1)
+    forwarded = passed_along(block_out[None, None], "pipe", 1)
     head_rows = lax.dynamic_index_in_dim(head_mod, step_row, 0, keepdims=False)
     normed_out = modulate(block_out, head_rows[0], head_rows[1]).astype(jnp.bfloat16)
     readout = jnp.dot(normed_out, head_weight, preferred_element_type=jnp.float32)
@@ -235,7 +252,7 @@
     unconditional = jnp.where(branch_index == 0, partner, readout)
     combined = unconditional + guidance * (conditional - unconditional)
     guided = lax.dynamic_slice_in_dim(combined, branch_index * half_width, half_width, 1)
-    return (forwarded[None, None], fresh_pair[None, None], guided[None])
+    return (forwarded, fresh_pair[None, None], guided[None])
 
 
 def solution(mesh):

time: 401 us -> 352 us (0.88)
  waiting for transfers between devices: 220 us -> 184 us
  Pallas kernels: 71.8 us -> 64.8 us
  local copies, waits for them, and re-layouts: 30.4 us -> 24.5 us
    all_gather x1, waiting for transfers between devices: 47.6 us -> 0.99 us  [per_device(): own_weights = lax.all_gather(mine, 'x', axis=0)]
    ppermute x10, waiting for transfers between devices: 32.3 us -> 53.7 us  [passed_along(): return lax.ppermute(block, axis, route)]
    all_gather x1, waiting for transfers between devices: 133 us -> 122 us  [per_device(): gathered = lax.all_gather(normed, ('y', 'x'), axis=0, tiled=True)]
    pallas_call x4 -> x3, Pallas kernels: 31.7 us -> 24.7 us  [project(): pl.pallas_call(functools.partial(project_body, sources=count, groups=grou...]
    slice x3 -> x0, local copies, waits for them, and re-layouts: 4.68 us -> none  [the longest x1 2.42 us: per_device(): from_below = passed_along(across[:cut], 'y', 1)]
  transfers between devices with their start and end apart: 18 -> 18, of which waited for: 11 -> 11; matrix products, arithmetic and copies ran while one was open for 14% -> 15% of each run, Pallas kernels for 15% -> 15%
where the time goes in v3:
time: 352 us; the launch traced here: 351 us
  waiting for transfers between devices  184 us (52%)
  Pallas kernels  64.8 us (18%)
  starting transfers between devices  24.8 us (7%)
  local copies, waits for them, and re-layouts  24.5 us (7%)
  matrix products  21.6 us (6%)
  between operations  15.8 us (4%)
  other arithmetic  14.5 us (4%)
    all_gather x1, waiting for transfers between devices, per_device(): gathered = lax.all_gather(normed, ('y', 'x'), axis=0, tiled=True)  122 us
    ppermute x10, waiting for transfers between devices, passed_along(): return lax.ppermute(block, axis, route)  53.7 us
    pallas_call x4, Pallas kernels, attend(): pl.pallas_call(attend_body, grid_spec=pltpu.PrefetchScalarGridSpec(num_sc...  35.8 us
    pallas_call x3, Pallas kernels, project(): pl.pallas_call(functools.partial(project_body, sources=count, groups=grou...  24.7 us
    dot_general x1, matrix products, per_device(): jnp.dot(gathered, in_weight, preferred_element_type=jnp.float32)  20.9 us
    unnamed x29, local copies, waits for them, and re-layouts  18.3 us
    ppermute x10, starting transfers between devices, passed_along(): return lax.ppermute(block, axis, route)  15.4 us
    ppermute x6, starting transfers between devices, partner_2(): lax.ppermute(shard, axis, [(i, i ^ stride) for i in range(lax.axis_size(a...  9.29 us
  transfers between devices with their start and end apart: 18, of which 11 were waited for; matrix products, arithmetic and copies ran while one was open for 15% of the time, Pallas kernels for 15%

profile of v3, /device:TPU:0, one launch (start us, length us, event | category | flops | bytes accessed | tf_op | source)
XLA Modules:
  0.0 350.5 jit_solution(3564385361264758573)
XLA Ops:
  9.7 4.3 %shard_map.121 = bf16[128,5120]{1,0:T(8,128)(2,1)} custom-call(bf16[128,5120]{1,0:T(8,128)(2,1)} %bitcast.78, f32[3,5120]{1,0:T(4,128)} %bitcast.80), custom_call_target="tpu_custom_call" | custom-call | tf_op jit(solution)/shard_map/pallas_call | solution.py:50
  14.1 10.7 %copy.13 = bf16[1,5120,3,256]{1,3,2,0:T(8,128)(2,1)} copy(bf16[1,5120,3,256]{3,1,2,0:T(8,128)(2,1)} %param.11) | data formatting | bytes 15728640 | tf_op args[1]
  24.7 2.6 dynamic-slice_bitcast_fusion
  27.4 121.9 %all-gather.4.cloned.1.call-done = bf16[2048,5120]{1,0:T(8,128)(2,1)} async-done(((bf16[128,5120]{1,0:T(8,128)(2,1)}), bf16[2048,5120]{1,0:T(8,128)(2,1)}) %all-gather.4.cloned.1.call-update) | async-done | bytes 20971536 | tf_op jit(solution)/shard_map/all_gather | solution.py:185
  149.2 20.9 %fusion.24 = f32[2048,768]{1,0:T(8,128)S(1)} fusion(bf16[2048,5120]{1,0:T(8,128)(2,1)} %all-gather.4.cloned.1.call-done, bf16[5120,768]{0,1:T(8,128)(2,1)} %bitcast.79), kind=kOutput, calls=%fused_computation.52 | convolution fusion | flops 16106127360 | bytes 35127296 | tf_op jit(solution)/shard_map/dot_general | solution.py:191
  170.1 2.6 copy-done.4
  174.9 2.6 collective-permute-done
  177.6 3.1 collective-permute-start.1
  187.1 3.1 collective-permute-start.3
  192.4 3.3 fusion.12
  195.8 2.3 fusion.19
  198.0 8.9 %shard_map.124 = bf16[512,256]{1,0:T(8,128)(2,1)} custom-call(s32[2]{0:T(128)} %pad_add_fusion.2.where_ref, bf16[4,512,256]{2,1,0:T(8,128)(2,1)} %bitcast.72, bf16[2,2048,256]{2,1,0:T(8,128)(2,1)} %get-tuple-element.32.kf.vf, bf16[2,2048,256]{2,1,0:T(8,128)(2,1)} %get-tuple-element.32.kf.vf, bf16[2,4096,256]{2,1,0:T(8,128)(2,1)} %bitcast.64, ...), custom_call_target="tpu_custom_call" | custom-call | flops 2147483648 | bytes 4194304 | tf_op jit(solution)/shard_map/pallas_call | solution.py:86
  210.6 2.8 collective-permute-start.5
  213.5 9.0 %shard_map.125 = bf16[512,256]{1,0:T(8,128)(2,1)} custom-call(s32[2]{0:T(128)} %pad_add_fusion.3.where_ref, bf16[4,512,256]{2,1,0:T(8,128)(2,1)} %bitcast.73, bf16[2,2048,256]{2,1,0:T(8,128)(2,1)} %get-tuple-element.32.kf.vf, bf16[2,2048,256]{2,1,0:T(8,128)(2,1)} %get-tuple-element.32.kf.vf, bf16[2,4096,256]{2,1,0:T(8,128)(2,1)} %bitcast.66, ...), custom_call_target="tpu_custom_call" | custom-call | flops 2147483648 | bytes 4194304 | tf_op jit(solution)/shard_map/pallas_call | solution.py:86
  223.5 9.0 %shard_map.123 = bf16[512,256]{1,0:T(8,128)(2,1)} custom-call(s32[2]{0:T(128)} %pad_add_fusion.1.where_ref, bf16[4,512,256]{2,1,0:T(8,128)(2,1)} %bitcast.74, bf16[2,2048,256]{2,1,0:T(8,128)(2,1)} %get-tuple-element.32.kf.vf, bf16[2,2048,256]{2,1,0:T(8,128)(2,1)} %get-tuple-element.32.kf.vf, bf16[2,4096,256]{2,1,0:T(8,128)(2,1)} %bitcast.68, ...), custom_call_target="tpu_custom_call" | custom-call | flops 2147483648 | bytes 4194304 | tf_op jit(solution)/shard_map/pallas_call | solution.py:86
  234.0 8.9 %shard_map.122.refs_0_.refs_1_.refs_8_.refs_9_ = bf16[512,256]{1,0:T(8,128)(2,1)} custom-call(s32[2]{0:T(128)} %pad_add_fusion.where_ref, bf16[4,512,256]{2,1,0:T(8,128)(2,1)} %bitcast.75, bf16[2,2048,256]{2,1,0:T(8,128)(2,1)} %get-tuple-element.32.kf.vf, bf16[2,2048,256]{2,1,0:T(8,128)(2,1)} %get-tuple-element.32.kf.vf, bf16[2,4096,256]{2,1,0:T(8,128)(2,1)} %bitcast.70, ...), custom_call_target="tpu_custom_call" | custom-call | flops 2147483648 | bytes 4194304 | tf_op jit(solution)/shard_map/pallas_call | solution.py:86
  243.9 7.9 %shard_map.128 = (bf16[64,5120]{1,0:T(8,128)(2,1)}, bf16[64,5120]{1,0:T(8,128)(2,1)}) custom-call(s32[6]{0:T(128)} %stack.81.where_ref, bf16[512,256]{1,0:T(8,128)(2,1)} %shard_map.122.refs_0_.refs_1_.refs_8_.refs_9_, bf16[512,256]{1,0:T(8,128)(2,1)} %shard_map.122.refs_0_.refs_1_.refs_8_.refs_9_, bf16[512,256]{1,0:T(8,128)(2,1)} %copy-done.3, ...), custom_call_target="tpu_custom_call" | custom-call | flops 1342177280 | bytes 10485760 | tf_op jit(solution)/shard_map/pallas_call | solution.py:143
  254.6 9.0 %shard_map.127 = (bf16[64,5120]{1,0:T(8,128)(2,1)}, bf16[64,5120]{1,0:T(8,128)(2,1)}, bf16[64,5120]{1,0:T(8,128)(2,1)}, bf16[64,5120]{1,0:T(8,128)(2,1)}) custom-call(s32[7]{0:T(128)} %stack.79.where_ref, bf16[512,256]{1,0:T(8,128)(2,1)} %shard_map.122.refs_0_.refs_1_.refs_8_.refs_9_, bf16[512,256]{1,0:T(8,128)(2,1)} %shard_map.122.refs_0_.refs_1_.refs_8_.refs_9_, ...), custom_call_target="tpu_custom_call" | custom-call | flops 2684354560 | bytes 10485760 | tf_op jit(solution)/shard_map/pallas_call | solution.py:143
  267.6 7.9 %shard_map.126 = (bf16[64,5120]{1,0:T(8,128)(2,1)}, bf16[64,5120]{1,0:T(8,128)(2,1)}) custom-call(s32[6]{0:T(128)} %stack.70.where_ref, bf16[512,256]{1,0:T(8,128)(2,1)} %shard_map.122.refs_0_.refs_1_.refs_8_.refs_9_, bf16[512,256]{1,0:T(8,128)(2,1)} %shard_map.122.refs_0_.refs_1_.refs_8_.refs_9_, bf16[512,256]{1,0:T(8,128)(2,1)} %copy-done.3, ...), custom_call_target="tpu_custom_call" | custom-call | flops 1342177280 | bytes 10485760 | tf_op jit(solution)/shard_map/pallas_call | solution.py:143
  277.3 16.8 %collective-permute-done.12 = bf16[64,5120]{1,0:T(8,128)(2,1)S(1)} collective-permute-done((bf16[64,5120]{1,0:T(8,128)(2,1)S(1)}, bf16[64,5120]{1,0:T(8,128)(2,1)S(1)}, u32[]{:S(2)}, u32[]{:S(2)}) %collective-permute-start.12) | collective-permute-done | bytes 655392 | tf_op jit(solution)/shard_map/ppermute | solution.py:22
  294.3 3.0 collective-permute-start.13
  298.3 11.6 %collective-permute-done.13 = bf16[64,5120]{1,0:T(8,128)(2,1)S(1)} collective-permute-done((bf16[64,5120]{1,0:T(8,128)(2,1)S(1)}, bf16[64,5120]{1,0:T(8,128)(2,1)S(1)}, u32[]{:S(2)}, u32[]{:S(2)}) %collective-permute-start.13) | collective-permute-done | bytes 655392 | tf_op jit(solution)/shard_map/ppermute | solution.py:22
  316.7 24.5 %collective-permute-done.14 = bf16[1,1,128,5120]{3,2,1,0:T(8,128)(2,1)} collective-permute-done((bf16[1,1,128,5120]{3,2,1,0:T(8,128)(2,1)}, bf16[1,1,128,5120]{3,2,1,0:T(8,128)(2,1)}, u32[]{:S(2)}, u32[]{:S(2)}) %collective-permute-start.14) | collective-permute-done | bytes 1310752 | tf_op jit(solution)/shard_map/ppermute | solution.py:22
  341.2 2.5 copy.20
  (85 shorter events, 35.8 us)
Async XLA Ops:
  7.2 142.0 %all-gather.4.cloned.1.call-start = ((), (), s32[]{:S(2)}) async-start(), calls=%async_computation | async-start | bytes 22282240 | tf_op jit(solution)/shard_map/all_gather | solution.py:185
  14.0 194.0 %all-gather.6.cloned.1.call-start = ((), (), s32[]{:S(2)}) async-start(), calls=%async_computation.1 | async-start | bytes 6553600 | tf_op jit(solution)/shard_map/all_gather | solution.py:190
  173.4 4.1 %collective-permute-start = (f32[2,2048]{1,0:T(2,128)S(1)}, f32[2,2048]{1,0:T(2,128)S(1)}, u32[]{:S(2)}, u32[]{:S(2)}) collective-permute-start(f32[2,2048]{1,0:T(2,128)S(1)} %pad_maximum_fusion.1), channel_id=1, source_target_pairs={{0,2},{2,0},{4,6},{6,4},{1,3},{3,1},{5,7},{7,5},{8,10},{10,8},{12,... | collective-permute-start | bytes 49160 | tf_op jit(solution)/shard_map/ppermute | solution.py:26
  177.6 5.6 %collective-permute-start.1 = (f32[2,2048]{1,0:T(2,128)S(1)}, f32[2,2048]{1,0:T(2,128)S(1)}, u32[]{:S(2)}, u32[]{:S(2)}) collective-permute-start(f32[2,2048]{1,0:T(2,128)S(1)} %fusion.18), channel_id=1, source_target_pairs={{0,4},{2,6},{4,0},{6,2},{1,5},{3,7},{5,1},{7,3},{8,12},{10,14},{12... | collective-permute-start | bytes 49160 | tf_op jit(solution)/shard_map/ppermute | solution.py:26
  183.2 3.8 %collective-permute-start.2 = (f32[2,2048]{1,0:T(2,128)S(1)}, f32[2,2048]{1,0:T(2,128)S(1)}, u32[]{:S(2)}, u32[]{:S(2)}) collective-permute-start(f32[2,2048]{1,0:T(2,128)S(1)} %fusion.28), channel_id=1, source_target_pairs={{0,8},{8,0},{16,24},{24,16},{1,9},{9,1},{17,25},{25,17},{2,10},{10... | collective-permute-start | bytes 49160 | tf_op jit(solution)/shard_map/ppermute | solution.py:26
  187.1 5.3 %collective-permute-start.3 = (f32[2,2048]{1,0:T(2,128)S(1)}, f32[2,2048]{1,0:T(2,128)S(1)}, u32[]{:S(2)}, u32[]{:S(2)}) collective-permute-start(f32[2,2048]{1,0:T(2,128)S(1)} %add.163), channel_id=1, source_target_pairs={{0,16},{8,24},{16,0},{24,8},{1,17},{9,25},{17,1},{25,9},{2,18},{10... | collective-permute-start | bytes 49160 | tf_op jit(solution)/shard_map/ppermute | solution.py:26
  208.0 35.0 %collective-permute-start.7 = (bf16[4,128,5120]{2,1,0:T(8,128)(2,1)}, bf16[4,128,5120]{2,1,0:T(8,128)(2,1)}, u32[]{:S(2)}, u32[]{:S(2)}) collective-permute-start(bf16[4,128,5120]{2,1,0:T(8,128)(2,1)} %bitcast.51), channel_id=1, source_target_pairs={{0,1},{1,0},{2,3},{3,2},{4,5},{5,4},{6,7},{7,6},{8,9},{9,8},{10,11... | collective-permute-start | bytes 15728648 | tf_op jit(solution)/shard_map/ppermute | solution.py:26
  210.6 32.4 %collective-permute-start.5 = (bf16[512,256]{1,0:T(8,128)(2,1)}, bf16[512,256]{1,0:T(8,128)(2,1)S(1)}, u32[]{:S(2)}, u32[]{:S(2)}) collective-permute-start(bf16[512,256]{1,0:T(8,128)(2,1)} %shard_map.124), channel_id=1, source_target_pairs={{4,0},{6,2},{0,4},{2,6},{5,1},{7,3},{1,5},{3,7},{12,8},{14,10},{8,... | collective-permute-start | bytes 786440 | tf_op jit(solution)/shard_map/ppermute | solution.py:22
  222.4 20.5 %collective-permute-start.6 = (bf16[512,256]{1,0:T(8,128)(2,1)}, bf16[512,256]{1,0:T(8,128)(2,1)S(1)}, u32[]{:S(2)}, u32[]{:S(2)}) collective-permute-start(bf16[512,256]{1,0:T(8,128)(2,1)} %shard_map.125), channel_id=1, source_target_pairs={{2,0},{4,2},{6,4},{0,6},{3,1},{5,3},{7,5},{1,7},{10,8},{12,10},{14... | collective-permute-start | bytes 786440 | tf_op jit(solution)/shard_map/ppermute | solution.py:22
  232.5 10.5 %collective-permute-start.4 = (bf16[512,256]{1,0:T(8,128)(2,1)}, bf16[512,256]{1,0:T(8,128)(2,1)S(1)}, u32[]{:S(2)}, u32[]{:S(2)}) collective-permute-start(bf16[512,256]{1,0:T(8,128)(2,1)} %shard_map.123), channel_id=1, source_target_pairs={{6,0},{0,2},{2,4},{4,6},{7,1},{1,3},{3,5},{5,7},{14,8},{8,10},{10,... | collective-permute-start | bytes 786440 | tf_op jit(solution)/shard_map/ppermute | solution.py:22
  251.8 23.8 %collective-permute-start.8 = (bf16[64,5120]{1,0:T(8,128)(2,1)}, bf16[64,5120]{1,0:T(8,128)(2,1)}, u32[]{:S(2)}, u32[]{:S(2)}) collective-permute-start(bf16[64,5120]{1,0:T(8,128)(2,1)} %get-tuple-element.19), channel_id=1, source_target_pairs={{24,0},{0,8},{8,16},{16,24},{25,1},{1,9},{9,17},{17,25},{26,2},{2,... | collective-permute-start | bytes 1966088 | tf_op jit(solution)/shard_map/ppermute | solution.py:22
  254.6 11.0 %copy-start.12 = (bf16[64,5120]{1,0:T(8,128)(2,1)S(1)}, bf16[64,5120]{1,0:T(8,128)(2,1)}, u32[]{:S(2)}) copy-start(bf16[64,5120]{1,0:T(8,128)(2,1)} %get-tuple-element.24) | copy-start | bytes 1966084
  263.5 33.8 %collective-permute-start.10 = (bf16[64,5120]{1,0:T(8,128)(2,1)}, bf16[64,5120]{1,0:T(8,128)(2,1)S(1)}, u32[]{:S(2)}, u32[]{:S(2)}) collective-permute-start(bf16[64,5120]{1,0:T(8,128)(2,1)} %get-tuple-element.20), channel_id=1, source_target_pairs={{8,0},{16,8},{24,16},{0,24},{9,1},{17,9},{25,17},{1,25},{10,2},{18... | collective-permute-start | bytes 1966088 | tf_op jit(solution)/shard_map/ppermute | solution.py:22
  265.6 28.5 %collective-permute-start.12 = (bf16[64,5120]{1,0:T(8,128)(2,1)S(1)}, bf16[64,5120]{1,0:T(8,128)(2,1)S(1)}, u32[]{:S(2)}, u32[]{:S(2)}) collective-permute-start(bf16[64,5120]{1,0:T(8,128)(2,1)S(1)} %copy-done.12), channel_id=1, source_target_pairs={{8,0},{16,8},{24,16},{0,24},{9,1},{17,9},{25,17},{1,25},{10,2},{18... | collective-permute-start | bytes 1966088 | tf_op jit(solution)/shard_map/ppermute | solution.py:22
  267.1 8.4 %copy-start.9 = (bf16[64,5120]{1,0:T(8,128)(2,1)S(1)}, bf16[64,5120]{1,0:T(8,128)(2,1)}, u32[]{:S(2)}) copy-start(bf16[64,5120]{1,0:T(8,128)(2,1)} %get-tuple-element.18) | copy-start | bytes 1966084
  267.1 31.2 %collective-permute-start.11 = (bf16[64,5120]{1,0:T(8,128)(2,1)}, bf16[64,5120]{1,0:T(8,128)(2,1)S(1)}, u32[]{:S(2)}, u32[]{:S(2)}) collective-permute-start(bf16[64,5120]{1,0:T(8,128)(2,1)} %get-tuple-element.22), channel_id=1, source_target_pairs={{24,0},{0,8},{8,16},{16,24},{25,1},{1,9},{9,17},{17,25},{26,2},{2,... | collective-permute-start | bytes 1966088 | tf_op jit(solution)/shard_map/ppermute | solution.py:22
  275.5 18.6 %copy-start.7 = (bf16[64,5120]{1,0:T(8,128)(2,1)S(1)}, bf16[64,5120]{1,0:T(8,128)(2,1)}, u32[]{:S(2)}) copy-start(bf16[64,5120]{1,0:T(8,128)(2,1)} %get-tuple-element.23) | copy-start | bytes 1966084
  275.5 22.5 %copy-start.8 = (bf16[64,5120]{1,0:T(8,128)(2,1)S(1)}, bf16[64,5120]{1,0:T(8,128)(2,1)}, u32[]{:S(2)}) copy-start(bf16[64,5120]{1,0:T(8,128)(2,1)} %get-tuple-element.17) | copy-start | bytes 1966084
  276.9 21.1 %collective-permute-start.9 = (bf16[64,5120]{1,0:T(8,128)(2,1)S(1)}, bf16[64,5120]{1,0:T(8,128)(2,1)S(1)}, u32[]{:S(2)}, u32[]{:S(2)}) collective-permute-start(bf16[64,5120]{1,0:T(8,128)(2,1)S(1)} %add_convert_fusion.1), channel_id=1, source_target_pairs={{24,0},{0,8},{8,16},{16,24},{25,1},{1,9},{9,17},{17,25},{26,2},{2,... | collective-permute-start | bytes 1966088 | tf_op jit(solution)/shard_map/ppermute | solution.py:22
  294.3 15.6 %copy-start.6 = (bf16[64,5120]{1,0:T(8,128)(2,1)S(1)}, bf16[64,5120]{1,0:T(8,128)(2,1)}, u32[]{:S(2)}) copy-start(bf16[64,5120]{1,0:T(8,128)(2,1)} %get-tuple-element.21) | copy-start | bytes 1966084
  294.3 15.6 %collective-permute-start.13 = (bf16[64,5120]{1,0:T(8,128)(2,1)S(1)}, bf16[64,5120]{1,0:T(8,128)(2,1)S(1)}, u32[]{:S(2)}, u32[]{:S(2)}) collective-permute-start(bf16[64,5120]{1,0:T(8,128)(2,1)S(1)} %add_convert_fusion), channel_id=1, source_target_pairs={{8,0},{16,8},{24,16},{0,24},{9,1},{17,9},{25,17},{1,25},{10,2},{18... | collective-permute-start | bytes 1966088 | tf_op jit(solution)/shard_map/ppermute | solution.py:22
  298.3 11.8 %copy-start.5 = (bf16[1,1,128,5120]{3,2,1,0:T(8,128)(2,1)S(1)}, bf16[1,1,128,5120]{3,2,1,0:T(8,128)(2,1)}, u32[]{:S(2)}) copy-start(bf16[1,1,128,5120]{3,2,1,0:T(8,128)(2,1)} %param.10) | copy-start | bytes 3932164
  311.5 29.7 %collective-permute-start.14 = (bf16[1,1,128,5120]{3,2,1,0:T(8,128)(2,1)}, bf16[1,1,128,5120]{3,2,1,0:T(8,128)(2,1)}, u32[]{:S(2)}, u32[]{:S(2)}) collective-permute-start(bf16[1,1,128,5120]{3,2,1,0:T(8,128)(2,1)} %fusion.7), channel_id=1, source_target_pairs={{96,0},{0,32},{32,64},{64,96},{97,1},{1,33},{33,65},{65,97},{98,2}... | collective-permute-start | bytes 3932168 | tf_op jit(solution)/shard_map/ppermute | solution.py:22
  314.9 1.3 collective-permute-start.15
  (7 other events, 17.3 us)
Sparse Core Ops, SparseCore 0:
  14.1 135.0 all-gather.3
  150.9 57.0 all-gather.5
